TPU v7x, 128 devices: a whole 4x4x4 slice. The times are simulated.
128 devices in a mesh: pb: 4 (over z_hi, core), ka: 32 (over z_lo, y, x).
Axes of the slice: x: 4, y: 4, z: 4 (z_hi: 2, z_lo: 2; z = z_hi * 2 + z_lo), core: 2. Of those that a mesh axis runs over, the one named last changes fastest.
Arguments:
- vertex_ladder: float32 [2, 16, 1024, 1024], P(None, 'pb', 'ka'), may hold values from -6 to 6
- vertex_cross_a: float32 [2, 16, 1024, 1024], P(None, 'pb', 'ka'), may hold values from -6 to 6
- vertex_cross_b: float32 [2, 16, 1024, 1024], P(None, 'pb', 'ka'), may hold values from -6 to 6
- bubble: float32 [2, 16, 1024], P(None, 'pb'), may hold values from -0.072 to 0.072
- row_maps: int32 [2, 16, 1024], replicated, may hold values from 0 to 16383, as said below
- col_maps: int32 [2, 1024], replicated, may hold values from 0 to 1023, each once within a row
Outputs:
- ladder_out: float32 [2, 16, 1024, 1024], P(None, 'pb', 'ka')
- crossed_a: float32 [2, 16, 1024, 1024], P(None, 'pb', 'ka')
- crossed_b: float32 [2, 16, 1024, 1024], P(None, 'pb', 'ka')
Inputs may be any that keep to these rules, and one draw needn't show every extreme that they name: `row_maps`: each of the two maps is a permutation of all 16384 rows. A device holds the rows of its bosonic indices (index of pb) and its first fermionic indices (index of ka); the 128 rows of one device take exactly 1 of their source rows from each device.
All inputs are finite; a program needn't handle non-finite values.
Results may differ from a plain program's by a relative error of at most 0.007.
Values may be sent and summed in bfloat16 or wider, within the bound.
A program may use at most 64 MiB of HBM per device.

v0:
```python
import jax
import jax.numpy as jnp
from jax import lax
from jax.sharding import PartitionSpec as P

LADDER = 6


def in_one_piece(arrays, axis, split_dim, concat_dim, along):
    ends, at = ([], 0)
    for a in arrays[:-1]:
        at += a.shape[along]
        ends.append(at)
    both = jnp.concatenate(arrays, axis=along)
    return tuple(
        jnp.split(
            lax.all_to_all(both, axis, split_axis=split_dim, concat_axis=concat_dim, tiled=True),
            ends,
            axis=along,
        )
    )


def ladder_rows(vertex_rows, bubble_q, gathered):
    col_count = gathered.shape[2]
    row_count = vertex_rows.shape[1]
    right_op = jnp.concatenate([gathered[0], gathered[1]], 1)
    current = vertex_rows
    for _ in range(LADDER):
        scaled_re = current[0] * bubble_q[0][None, :] - current[1] * bubble_q[1][None, :]
        scaled_im = current[0] * bubble_q[1][None, :] + current[1] * bubble_q[0][None, :]
        left_op = jnp.concatenate([scaled_re, scaled_im], 0).astype(jnp.bfloat16)
        product = jnp.dot(left_op, right_op, preferred_element_type=jnp.float32)
        real_part = product[:row_count, :col_count] - product[row_count:, col_count:]
        imag_part = product[:row_count, col_count:] + product[row_count:, :col_count]
        current = vertex_rows + jnp.stack([real_part, imag_part])
    return current


def per_device(vertex_ladder, vertex_cross_a, vertex_cross_b, bubble, row_maps, col_maps):
    q_local = vertex_ladder.shape[1]
    row_count = vertex_ladder.shape[2]
    col_count = vertex_ladder.shape[3]
    gamma_low = vertex_ladder.astype(jnp.bfloat16)
    whole_low = lax.all_gather(gamma_low, "ka", axis=2, tiled=True)

    def per_whole(loop_state, scan_items):
        vertex_rows, gathered, bubble_q = scan_items
        return (loop_state, ladder_rows(vertex_rows, bubble_q, gathered))

    _, stacked = lax.scan(
        per_whole,
        jnp.int32(0),
        (
            jnp.moveaxis(vertex_ladder, 1, 0),
            jnp.moveaxis(whole_low, 1, 0),
            jnp.moveaxis(bubble, 1, 0),
        ),
    )
    ladder_out = jnp.moveaxis(stacked, 0, 1)
    local_count = q_local * row_count
    reducible = (ladder_out - vertex_ladder).reshape(2, local_count, col_count)
    pb_count = lax.axis_size("pb")
    ka_count = lax.axis_size("ka")
    dev_count = pb_count * ka_count
    per_peer = local_count // dev_count
    my_device = lax.axis_index("pb") * ka_count + lax.axis_index("ka")
    my_bos = lax.axis_index("pb") * q_local + jnp.arange(q_local, dtype=jnp.int32)
    my_fer = lax.axis_index("ka") * row_count + jnp.arange(row_count, dtype=jnp.int32)
    my_rows = (my_bos[:, None] * col_count + my_fer[None, :]).reshape(-1)
    slot_ids = jnp.arange(per_peer, dtype=jnp.int32)

    def device_of(global_rows):
        return global_rows // col_count // q_local * ka_count + global_rows % col_count // row_count

    def prepare(table_flat):
        by_device = (
            table_flat.reshape(pb_count, q_local, ka_count, row_count)
            .transpose(0, 2, 1, 3)
            .reshape(dev_count, local_count)
        )
        mine = (device_of(by_device) == my_device).astype(jnp.int32)
        rank = jnp.cumsum(mine, 1) - 1
        source_local = (
            by_device // col_count % q_local * row_count + by_device % col_count % row_count
        )
        hits = mine[:, :, None] * (rank[:, :, None] == slot_ids[None, None, :]).astype(jnp.int32)
        send_index = jnp.sum(hits * source_local[:, :, None], 1).reshape(-1)
        return jnp.take(reducible, send_index, axis=1)

    def place(table_flat, received, column_map):
        source = table_flat[my_rows]
        source_dev = device_of(source)
        onehot = (source_dev[:, None] == jnp.arange(dev_count, dtype=jnp.int32)[None, :]).astype(
            jnp.int32
        )
        slot_index = jnp.sum((jnp.cumsum(onehot, 0) - onehot) * onehot, 1)
        picked = jnp.take(received, source_dev * per_peer + slot_index, axis=1)
        selector = (jnp.arange(col_count, dtype=jnp.int32)[:, None] == column_map[None, :]).astype(
            jnp.float32
        )
        picked = jnp.einsum("prk,km->prm", picked, selector, precision=lax.Precision.HIGHEST)
        return picked.reshape(2, q_local, row_count, col_count)

    table_a = row_maps[0].reshape(-1)
    table_b = row_maps[1].reshape(-1)
    send_a = prepare(table_a)
    send_b = prepare(table_b)
    recv_a, recv_b = in_one_piece((send_a, send_b), ("pb", "ka"), 1, 1, 0)
    crossed_a = vertex_cross_a + place(table_a, recv_a, col_maps[0])
    crossed_b = vertex_cross_b + place(table_b, recv_b, col_maps[1])
    return (ladder_out, crossed_a, crossed_b)


def solution(mesh):
    return jax.shard_map(
        per_device,
        mesh=mesh,
        in_specs=(
            P(None, "pb", "ka", None),
            P(None, "pb", "ka", None),
            P(None, "pb", "ka", None),
            P(None, "pb", None),
            P(),
            P(),
        ),
        out_specs=(P(None, "pb", "ka", None), P(None, "pb", "ka", None), P(None, "pb", "ka", None)),
        check_vma=False,
    )
```

profile of v0, /device:TPU:1, one launch (start us, length us, event | category | flops | bytes accessed | tf_op | source)
XLA Modules:
  0.0 306.2 jit_solution(12772516117283020420)
XLA Ops:
  7.2 2.1 copy.49
  9.4 1.3 copy.50
  13.1 4.7 %fusion.64 = (s32[4,32]{1,0:T(4,128)S(1)}, s32[4,32]{1,0:T(4,128)S(1)}) fusion(pred[4,32,4,32]{3,2,1,0:T(4,128)(4,1)S(1)} %eq.118, s32[]{:T(128)S(6)} %add.312, s32[4,4,32,32]{3,2,1,0:T(8,128)S(1)} %reshape_reshape_squeeze.7, pred[4,32,4,32]{3,2,1,0:T(4,128)(4,1)S(1)} %eq.113, s32[4,4,32,32]{3,2,1,0:T(8,128)S(1)} %reshape_reshape_squeeze.6), kind=kLoop, calls=%fused_computation.162 | loop fusion | flops 2162432 | bytes 164868 | tf_op jit(solution)/shard_map/reduce_sum | solution.py:88
  18.2 183.1 %all-gather.2.cloned.1.call-done = bf16[2,4,1024,1024]{3,2,0,1:T(8,128)(2,1)} async-done(((bf16[2,4,32,1024]{3,2,0,1:T(8,128)(2,1)}), bf16[2,4,1024,1024]{3,2,0,1:T(8,128)(2,1)}) %all-gather.2.cloned.1.call-update) | async-done | bytes 16777232 | tf_op jit(solution)/shard_map/all_gather | solution.py:45
  201.3 34.4 %while.10 = (s32[]{:T(128)}, f32[4,2,32,1024]{3,2,0,1:T(8,128)S(1)}, f32[4,2,32,1024]{3,2,1,0:T(8,128)S(1)}, f32[4,2,1024]{2,1,0:T(2,128)S(1)}, bf16[4,2,1024,10...) while((s32[]{:T(128)}, f32[4,2,32,1024]{3,2,0,1:T(8,128)S(1)}, f32[4,2,32,1024]{3,2,1,0:T(8,128)S(1)}, ...), condition=%wide.region_1.2_spmd, body=%wide.region_0.1_spmd.sunk | while | flops 1665269760 | bytes 49348760 | solution.py:51
  201.4 2.7 dynamic-slice_bitcast_fusion.5
  209.0 0.8 fusion.134
  210.1 2.7 dynamic-slice_bitcast_fusion.5
  218.7 2.7 dynamic-slice_bitcast_fusion.5
  227.2 2.7 dynamic-slice_bitcast_fusion.5
  236.8 1.7 gather_fusion.3
  238.5 1.7 gather_fusion.2
  241.2 2.3 pad_maximum_fusion.7
  243.5 12.0 %all-to-all-start = ((f32[4,128,1024]{2,0,1:T(4,128)}), f32[4,128,1024]{2,0,1:T(4,128)S(1)}, u32[]{:S(2)}, u32[]{:S(2)}) async-start(f32[4,128,1024]{2,0,1:T(4,128)} %pad_maximum_fusion.7), calls=%async_computation | async-start | bytes 4194304 | tf_op jit(solution)/shard_map/all_to_all | solution.py:17
  255.5 1.1 gather_fusion
  257.0 1.1 gather_fusion.1
  258.9 25.9 %all-to-all-done = f32[4,128,1024]{2,0,1:T(4,128)S(1)} async-done(((f32[4,128,1024]{2,0,1:T(4,128)}), f32[4,128,1024]{2,0,1:T(4,128)S(1)}, u32[]{:S(2)}, u32[]{:S(2)}) %all-to-all-start) | async-done | bytes 2097184 | tf_op jit(solution)/shard_map/all_to_all | solution.py:17
  284.8 1.8 fusion.97
  286.6 3.0 gather_fusion.4
  290.1 2.3 fusion.45
  292.5 1.1 add.337
  293.6 1.7 gather_fusion.5
  295.8 2.3 fusion.48
  298.2 1.1 add.341
  (171 shorter events, 28.9 us)
Async XLA Ops:
  7.2 3.5 %copy-start.5 = (f32[2,4,1024]{2,1,0:T(4,128)S(1)}, f32[2,4,1024]{2,1,0:T(4,128)}, u32[]{:S(2)}) copy-start(f32[2,4,1024]{2,1,0:T(4,128)} %param.13) | copy-start | bytes 98308
  7.2 3.6 %copy-start.4 = (s32[2,16,1024]{2,1,0:T(8,128)S(1)}, s32[2,16,1024]{2,1,0:T(8,128)}, u32[]{:S(2)}) copy-start(s32[2,16,1024]{2,1,0:T(8,128)} %param.14) | copy-start | bytes 393220
  7.2 194.1 %all-gather.2.cloned.1.call-start = ((), (), s32[]{:S(2)}) async-start(), calls=%async_computation.1 | async-start | bytes 17301504 | tf_op jit(solution)/shard_map/all_gather | solution.py:45
  201.3 34.5 %copy-start = (f32[2,4,32,1024]{3,2,1,0:T(8,128)S(1)}, f32[2,4,32,1024]{3,2,1,0:T(8,128)}, u32[]{:S(2)}) copy-start(f32[2,4,32,1024]{3,2,1,0:T(8,128)} %param.10) | copy-start | bytes 3145732
  235.8 1.0 copy-start.3
  241.2 17.6 %copy-start.6 = (s32[2,1024]{1,0:T(2,128)S(1)}, s32[2,1024]{1,0:T(2,128)}, u32[]{:S(2)}) copy-start(s32[2,1024]{1,0:T(2,128)} %param.15) | copy-start | bytes 24580
  243.5 41.3 %all-to-all-start = ((f32[4,128,1024]{2,0,1:T(4,128)}), f32[4,128,1024]{2,0,1:T(4,128)S(1)}, u32[]{:S(2)}, u32[]{:S(2)}) async-start(f32[4,128,1024]{2,0,1:T(4,128)} %pad_maximum_fusion.7), calls=%async_computation | async-start | bytes 4194304 | tf_op jit(solution)/shard_map/all_to_all | solution.py:17
  286.6 5.9 %copy-start.1 = (f32[2,4,32,1024]{3,2,1,0:T(8,128)S(1)}, f32[2,4,32,1024]{3,2,1,0:T(8,128)}, u32[]{:S(2)}) copy-start(f32[2,4,32,1024]{3,2,1,0:T(8,128)} %param.11) | copy-start | bytes 3145732
  293.6 4.6 %copy-start.2 = (f32[2,4,32,1024]{3,2,1,0:T(8,128)S(1)}, f32[2,4,32,1024]{3,2,1,0:T(8,128)}, u32[]{:S(2)}) copy-start(f32[2,4,32,1024]{3,2,1,0:T(8,128)} %param.12) | copy-start | bytes 3145732
Sparse Core Ops, SparseCore 0:
  10.2 191.0 all-gather.1
where the time goes:
time: 306 us
  waiting for transfers between devices  209 us (68%)
  local copies, waits for them, and re-layouts  29 us (9%)
  matrix products  24.9 us (8%)
  other arithmetic  15.9 us (5%)
  between operations  14.5 us (5%)
  starting transfers between devices  12 us (4%)
    all_gather x1, waiting for transfers between devices, per_device(): whole_low = lax.all_gather(gamma_low, 'ka', axis=2, tiled=True)  183 us
    all_to_all x1, waiting for transfers between devices, in_one_piece(): lax.all_to_all(both, axis, split_axis=split_dim, concat_axis=concat_dim,...  25.9 us
    dot_general x24, matrix products, ladder_rows(): product = jnp.dot(left_op, right_op, preferred_element_type=jnp.float32)  20.3 us
    all_to_all x1, starting transfers between devices, in_one_piece(): lax.all_to_all(both, axis, split_axis=split_dim, concat_axis=concat_dim,...  12 us
    squeeze x4, local copies, waits for them, and re-layouts, ladder_rows(): right_op = jnp.concatenate([gathered[0], gathered[1]], 1)  10.8 us
  transfers between devices with their start and end apart: 2, of which 2 were waited for; matrix products, arithmetic and copies ran while one was open for 4% of the time, Pallas kernels for 0%

commit v1 on v0

v1 whole, which is shorter than its diff:
```python
import jax
import jax.numpy as jnp
from jax import lax
from jax.experimental import pallas as pl
from jax.experimental.pallas import tpu as pltpu
from jax.sharding import PartitionSpec as P

LADDER = 6
MESH = pl.DeviceIdType.MESH
BF16 = jnp.bfloat16
F32 = jnp.float32
K = 1024
ROWS = 32
QL = 4
MINE = 4 * ROWS
NB = 256


def ladder_kernel(
    vertex_ref, bubble_ref, home_ref, low, whole, base, full, left_op, outgoing,
    chi, send1, send_chi, recv_chi, recv, send2, send3, send_home, recv_home,
):
    pb, ka = lax.axis_index("pb"), lax.axis_index("ka")
    z_hi, core = pb // 2, pb % 2
    z_lo, y, x = ka // 16, (ka // 4) % 4, ka % 4
    line = ka - x

    def taker(j):
        return (z_hi * 2 + 1 - z_lo, core * 16 + j * 4 + x)

    def giver(j):
        return (z_hi * 2 + z_lo, (1 - core) * 16 + j * 4 + x)

    right = (pb, line + (x + 1) % 4)
    left = (pb, line + (x + 3) % 4)
    partner = (z_hi * 2 + 1 - core, ka)

    barrier = pltpu.get_barrier_semaphore()
    for j in range(4):
        pl.semaphore_signal(barrier, inc=1, device_id=taker(j), device_id_type=MESH)
        pl.semaphore_signal(barrier, inc=1, device_id=giver(j), device_id_type=MESH)
    for other in (right, left, partner):
        pl.semaphore_signal(barrier, inc=1, device_id=other, device_id_type=MESH)
    for j in range(4):
        low[j] = vertex_ref[:, j].astype(BF16)
    pl.semaphore_wait(barrier, 11)

    def rows_of(piece):
        return pl.ds(pl.multiple_of(piece * ROWS, ROWS), ROWS)

    def copy1(j):
        return pltpu.make_async_remote_copy(
            src_ref=low.at[j],
            dst_ref=whole.at[:, rows_of(ka), :],
            send_sem=send1.at[j],
            recv_sem=recv.at[ka],
            device_id=taker(j),
            device_id_type=MESH,
        )

    def pass_on(piece, sem, target):
        block = whole.at[:, rows_of(piece), :]
        return pltpu.make_async_remote_copy(
            src_ref=block,
            dst_ref=block,
            send_sem=sem,
            recv_sem=recv.at[piece],
            device_id=target,
            device_id_type=MESH,
        )

    def piece_at(j, shift):
        return (1 - core) * 16 + j * 4 + (x + shift) % 4

    def chi_copy(j, slot):
        return pltpu.make_async_remote_copy(
            src_ref=bubble_ref.at[j],
            dst_ref=chi.at[slot],
            send_sem=send_chi.at[j],
            recv_sem=recv_chi.at[slot],
            device_id=taker(j),
            device_id_type=MESH,
        )

    for j in range(4):
        copy1(j).start()
        chi_copy(j, y).start()
    for j in range(4):
        piece = piece_at(j, 0)
        pass_on(piece, send2.at[j, 0], right).wait_recv()
        pass_on(piece, send2.at[j, 0], right).start()
        pass_on(piece, send2.at[j, 1], left).start()
        pass_on(piece, send3.at[j, 0], partner).start()
    for j in range(4):
        piece = piece_at(j, 3)
        pass_on(piece, send3.at[j, 1], partner).wait_recv()
        if j < 2:
            pass_on(piece, send2.at[j, 2], right).start()
        pass_on(piece, send3.at[j, 1], partner).start()
        piece = piece_at(j, 1)
        pass_on(piece, send3.at[j, 2], partner).wait_recv()
        if j >= 2:
            pass_on(piece, send2.at[j, 2], left).start()
        pass_on(piece, send3.at[j, 2], partner).start()
    for j in range(4):
        piece = piece_at(j, 2)
        pass_on(piece, send3.at[j, 3], partner).wait_recv()
        pass_on(piece, send3.at[j, 3], partner).start()

    for j in range(4):
        rows = whole[:, rows_of(piece_at(j, 0)), :].astype(F32)
        base[:, j * ROWS:(j + 1) * ROWS, :] = rows
        full[:, j * ROWS:(j + 1) * ROWS, :] = rows
    for i in range(16):
        pass_on(core * 16 + i, send3.at[0, 0], partner).wait_recv()

    for j in range(4):
        chi_copy(j, j).wait_recv()
    chi_re = chi[0, 0:1, :]
    chi_im = chi[0, 1:2, :]

    def scale(i, carry):
        rows = pl.ds(pl.multiple_of(i * ROWS, ROWS), ROWS)
        re, im = full[0, rows, :], full[1, rows, :]
        left_op[rows, :] = (re * chi_re - im * chi_im).astype(BF16)
        low_rows = pl.ds(pl.multiple_of(MINE + i * ROWS, ROWS), ROWS)
        left_op[low_rows, :] = (re * chi_im + im * chi_re).astype(BF16)
        return carry

    def product(cols):
        by_re = jnp.dot(left_op[...], whole[0, :, cols], preferred_element_type=F32)
        by_im = jnp.dot(left_op[...], whole[1, :, cols], preferred_element_type=F32)
        return by_re[:MINE] - by_im[MINE:], by_im[:MINE] + by_re[MINE:]

    def step(_, carry):
        lax.fori_loop(0, MINE // ROWS, scale, 0)

        def columns(n, inner):
            cols = pl.ds(pl.multiple_of(n * NB, NB), NB)
            re, im = product(cols)
            full[0, :, cols] = base[0, :, cols] + re
            full[1, :, cols] = base[1, :, cols] + im
            return inner

        return lax.fori_loop(0, K // NB, columns, carry)

    lax.fori_loop(0, LADDER - 1, step, 0)
    lax.fori_loop(0, MINE // ROWS, scale, 0)

    def last(n, carry):
        cols = pl.ds(pl.multiple_of(n * NB, NB), NB)
        re, im = product(cols)
        for j in range(4):
            outgoing[j, 0, :, cols] = re[j * ROWS:(j + 1) * ROWS].astype(BF16)
            outgoing[j, 1, :, cols] = im[j * ROWS:(j + 1) * ROWS].astype(BF16)
        return carry

    lax.fori_loop(0, K // NB, last, 0)

    def home_copy(j):
        return pltpu.make_async_remote_copy(
            src_ref=outgoing.at[j],
            dst_ref=home_ref.at[y],
            send_sem=send_home.at[j],
            recv_sem=recv_home.at[y],
            device_id=giver(j),
            device_id_type=MESH,
        )

    def from_home(j):
        return pltpu.make_async_remote_copy(
            src_ref=outgoing.at[j],
            dst_ref=home_ref.at[j],
            send_sem=send_home.at[j],
            recv_sem=recv_home.at[j],
            device_id=taker(j),
            device_id_type=MESH,
        )

    for j in range(4):
        home_copy(j).start()
    for j in range(4):
        copy1(j).wait_send()
        chi_copy(j, j).wait_send()
        for t in range(3):
            pass_on(piece_at(j, 0), send2.at[j, t], right).wait_send()
        for t in range(4):
            pass_on(piece_at(j, 0), send3.at[j, t], partner).wait_send()
    for j in range(4):
        from_home(j).wait_recv()
        home_copy(j).wait_send()


def run_ladder(vertex, bubble):
    vmem = pl.BlockSpec(memory_space=pltpu.VMEM)
    return pl.pallas_call(
        ladder_kernel,
        out_shape=jax.ShapeDtypeStruct((QL, 2, ROWS, K), BF16),
        in_specs=[vmem, vmem],
        out_specs=vmem,
        scratch_shapes=[
            pltpu.VMEM((QL, 2, ROWS, K), BF16),
            pltpu.VMEM((2, K, K), BF16),
            pltpu.VMEM((2, MINE, K), F32),
            pltpu.VMEM((2, MINE, K), F32),
            pltpu.VMEM((2 * MINE, K), BF16),
            pltpu.VMEM((QL, 2, ROWS, K), BF16),
            pltpu.VMEM((4, 2, K), F32),
            pltpu.SemaphoreType.DMA((4,)),
            pltpu.SemaphoreType.DMA((4,)),
            pltpu.SemaphoreType.DMA((4,)),
            pltpu.SemaphoreType.DMA((32,)),
            pltpu.SemaphoreType.DMA((4, 3)),
            pltpu.SemaphoreType.DMA((4, 4)),
            pltpu.SemaphoreType.DMA((4,)),
            pltpu.SemaphoreType.DMA((4,)),
        ],
        compiler_params=pltpu.CompilerParams(
            collective_id=0, has_side_effects=True, vmem_limit_bytes=40 * 2**20
        ),
    )(vertex, bubble)


def per_device(vertex_ladder, vertex_cross_a, vertex_cross_b, bubble, row_maps, col_maps):
    q_local = vertex_ladder.shape[1]
    row_count = vertex_ladder.shape[2]
    col_count = vertex_ladder.shape[3]
    pb_count = lax.axis_size("pb")
    ka_count = lax.axis_size("ka")
    dev_count = pb_count * ka_count
    local_count = q_local * row_count
    pb, ka = lax.axis_index("pb"), lax.axis_index("ka")
    home = run_ladder(vertex_ladder, jnp.moveaxis(bubble, 1, 0))
    home = jnp.moveaxis(home, 1, 0)
    ladder_out = vertex_ladder + home.astype(F32)
    reducible = home.reshape(2, local_count, col_count)
    my_device = pb * ka_count + ka
    my_bos = pb * q_local + jnp.arange(q_local, dtype=jnp.int32)
    my_fer = ka * row_count + jnp.arange(row_count, dtype=jnp.int32)

    def device_of(global_rows):
        return global_rows // col_count // q_local * ka_count + global_rows % col_count // row_count

    def prepare(table):
        by_device = (
            table.reshape(pb_count, q_local, ka_count, row_count)
            .transpose(0, 2, 1, 3)
            .reshape(dev_count, local_count)
        )
        mine = (device_of(by_device) == my_device).astype(jnp.int32)
        source_local = (
            by_device // col_count % q_local * row_count + by_device % col_count % row_count
        )
        send_index = jnp.sum(mine * source_local, 1)
        return jnp.take(reducible, send_index, axis=1)

    def place(table, received, column_map):
        source = lax.dynamic_slice(table, (pb * q_local, ka * row_count), (q_local, row_count))
        picked = jnp.take(received, device_of(source.reshape(-1)), axis=1)
        selector = (jnp.arange(col_count, dtype=jnp.int32)[:, None] == column_map[None, :]).astype(BF16)
        picked = jnp.einsum("prk,km->prm", picked, selector, preferred_element_type=F32)
        return picked.reshape(2, q_local, row_count, col_count)

    both = jnp.concatenate([prepare(row_maps[0]), prepare(row_maps[1])], axis=0)
    both = lax.all_to_all(both, ("pb", "ka"), split_axis=1, concat_axis=1, tiled=True)
    crossed_a = vertex_cross_a + place(row_maps[0], both[:2], col_maps[0])
    crossed_b = vertex_cross_b + place(row_maps[1], both[2:], col_maps[1])
    return (ladder_out, crossed_a, crossed_b)


def solution(mesh):
    return jax.shard_map(
        per_device,
        mesh=mesh,
        in_specs=(
            P(None, "pb", "ka", None),
            P(None, "pb", "ka", None),
            P(None, "pb", "ka", None),
            P(None, "pb", None),
            P(),
            P(),
        ),
        out_specs=(P(None, "pb", "ka", None), P(None, "pb", "ka", None), P(None, "pb", "ka", None)),
        check_vma=False,
    )
```

time: 306 us -> 102 us (0.33)
  waiting for transfers between devices: 209 us -> 15.3 us
  Pallas kernels: 0 us -> 53.9 us
  matrix products: 24.9 us -> 1.97 us
  local copies, waits for them, and re-layouts: 29 us -> 12.3 us
  between operations: 14.5 us -> 0.87 us
  other arithmetic: 15.9 us -> 9.33 us
  starting transfers between devices: 12 us -> 8.59 us
    all_gather x1 -> x0, waiting for transfers between devices: 183 us -> none  [per_device(): whole_low = lax.all_gather(gamma_low, 'ka', axis=2, tiled=True)]
    pallas_call x0 -> x1, Pallas kernels: none -> 53.9 us  [run_ladder(): pl.pallas_call(ladder_kernel, out_shape=jax.ShapeDtypeStruct((QL, 2, ROWS...]
    dot_general x26 -> x2, matrix products: 24.9 us -> 1.97 us  [place(): jnp.einsum('prk,km->prm', picked, selector, preferred_element_type=F32)]
    squeeze x4 -> x0, local copies, waits for them, and re-layouts: 10.8 us -> none  [ladder_rows(): right_op = jnp.concatenate([gathered[0], gathered[1]], 1)]
    all_to_all x1, waiting for transfers between devices: 25.9 us -> 15.3 us  [per_device(): lax.all_to_all(both, ('pb', 'ka'), split_axis=1, concat_axis=1, tiled=True)]
    gather x4 -> x2, local copies, waits for them, and re-layouts: 6.97 us -> 3.25 us  [place(): picked = jnp.take(received, device_of(source.reshape(-1)), axis=1)]
    reduce_sum x3 -> x1, other arithmetic: 5.05 us -> 1.56 us  [prepare(): send_index = jnp.sum(mine * source_local, 1)]
    all_to_all x1, starting transfers between devices: 12 us -> 8.59 us  [per_device(): lax.all_to_all(both, ('pb', 'ka'), split_axis=1, concat_axis=1, tiled=True)]
  transfers between devices with their start and end apart: 2 -> 1, of which waited for: 2 -> 1; matrix products, arithmetic and copies ran while one was open for 4% -> 4% of each run, Pallas kernels for 0% -> 0%
where the time goes in v1:
time: 102 us
  Pallas kernels  53.9 us (53%)
  waiting for transfers between devices  15.3 us (15%)
  local copies, waits for them, and re-layouts  12.3 us (12%)
  other arithmetic  9.33 us (9%)
  starting transfers between devices  8.59 us (8%)
  matrix products  1.97 us (2%)
    pallas_call x1, Pallas kernels, run_ladder(): pl.pallas_call(ladder_kernel, out_shape=jax.ShapeDtypeStruct((QL, 2, ROWS...  53.9 us
    all_to_all x1, waiting for transfers between devices, per_device(): lax.all_to_all(both, ('pb', 'ka'), split_axis=1, concat_axis=1, tiled=True)  15.3 us
    all_to_all x1, starting transfers between devices, per_device(): lax.all_to_all(both, ('pb', 'ka'), split_axis=1, concat_axis=1, tiled=True)  8.59 us
    gather x2, local copies, waits for them, and re-layouts, prepare(): return jnp.take(reducible, send_index, axis=1)  3.26 us
    gather x2, local copies, waits for them, and re-layouts, place(): picked = jnp.take(received, device_of(source.reshape(-1)), axis=1)  3.25 us
    unnamed x12, local copies, waits for them, and re-layouts  2.82 us
    concatenate x1, other arithmetic, per_device(): both = jnp.concatenate([prepare(row_maps[0]), prepare(row_maps[1])], axis=0)  2.05 us
  transfers between devices with their start and end apart: 1, of which 1 were waited for; matrix products, arithmetic and copies ran while one was open for 4% of the time, Pallas kernels for 0%

profile of v1, /device:TPU:1, one launch (start us, length us, event | category | flops | bytes accessed | tf_op | source)
XLA Modules:
  0.0 102.2 jit_solution(15669541237752435877)
XLA Ops:
  0.7 1.0 fusion.43
  1.9 1.6 %fusion.20 = (s32[4,32]{1,0:T(4,128)S(1)}, s32[4,32]{1,0:T(4,128)S(1)}) fusion(s32[4,4,32,32]{3,2,1,0:T(8,128)S(1)} %reshape_squeeze.6, s32[]{:T(128)S(6)} %add.115, s32[4,4,32,32]{3,2,1,0:T(8,128)S(1)} %reshape_squeeze.7), kind=kLoop, calls=%fused_computation.60 | loop fusion | flops 2096896 | bytes 132100 | tf_op jit(solution)/shard_map/reduce_sum | solution.py:254
  3.7 53.9 %shard_map.85 = bf16[4,2,32,1024]{3,2,1,0:T(8,128)(2,1)S(1)} custom-call(f32[2,4,32,1024]{3,2,1,0:T(8,128)S(1)} %copy-done, f32[4,2,1024]{2,1,0:T(2,128)S(1)} %bitcast.61), custom_call_target="tpu_custom_call" | custom-call | tf_op jit(solution)/shard_map/pallas_call | solution.py:196
  57.7 0.5 copy.15
  58.2 1.6 %gather_fusion.1 = bf16[128,2,1024]{2,1,0:T(2,128)(2,1)S(1)} fusion(bf16[2,128,1024]{2,0,1:T(2,128)(2,1)S(1)} %copy.15, s32[1024]{0:T(1024)S(1)} %pad_clamp_fusion.2), kind=kCustom, calls=%fused_computation.1.clone | custom fusion | bytes 1049088 | tf_op jit(solution)/shard_map/jit(_take)/gather | solution.py:255
  59.8 1.6 %gather_fusion = bf16[128,2,1024]{2,1,0:T(2,128)(2,1)S(1)} fusion(bf16[2,128,1024]{2,0,1:T(2,128)(2,1)S(1)} %copy.15, s32[1024]{0:T(1024)S(1)} %pad_clamp_fusion.3), kind=kCustom, calls=%fused_computation.clone | custom fusion | bytes 1049088 | tf_op jit(solution)/shard_map/jit(_take)/gather | solution.py:255
  61.5 0.6 fusion.10
  62.1 0.6 fusion.11
  62.6 2.1 %pad_maximum_fusion = bf16[4,128,1024]{2,0,1:T(4,128)(2,1)} fusion(bf16[2,128,1024]{2,0,1:T(2,128)(2,1)S(1)} %fusion.11, bf16[2,128,1024]{2,0,1:T(2,128)(2,1)S(1)} %fusion.10), kind=kLoop, calls=%fused_computation.12 | loop fusion | flops 2097152 | bytes 2097152 | tf_op jit(solution)/shard_map/concatenate | solution.py:264
  64.7 8.6 %all-to-all-start = ((bf16[4,128,1024]{2,0,1:T(4,128)(2,1)}), bf16[4,128,1024]{2,0,1:T(4,128)(2,1)S(1)}, u32[]{:S(2)}, u32[]{:S(2)}) async-start(bf16[4,128,1024]{2,0,1:T(4,128)(2,1)} %pad_maximum_fusion), calls=%async_computation | async-start | bytes 2097152 | tf_op jit(solution)/shard_map/all_to_all | solution.py:265
  73.3 1.1 %copy_add_fusion = f32[2,4,32,1024]{3,2,0,1:T(8,128)} fusion(f32[2,4,32,1024]{3,2,1,0:T(8,128)S(1)} %copy-done, bf16[4,2,32,1024]{3,2,1,0:T(8,128)(2,1)S(1)} %shard_map.85), kind=kLoop, calls=%fused_computation.13 | loop fusion | flops 524288 | bytes 2621440 | tf_op jit(solution)/shard_map/add | solution.py:235
  74.6 2.3 %copy.19 = f32[2,4,32,1024]{3,2,1,0:T(8,128)} copy(f32[2,4,32,1024]{3,2,0,1:T(8,128)} %copy_add_fusion) | data formatting | bytes 2097152
  77.1 15.3 %all-to-all-done = bf16[4,128,1024]{2,0,1:T(4,128)(2,1)S(1)} async-done(((bf16[4,128,1024]{2,0,1:T(4,128)(2,1)}), bf16[4,128,1024]{2,0,1:T(4,128)(2,1)S(1)}, u32[]{:S(2)}, u32[]{:S(2)}) %all-to-all-start) | async-done | bytes 1048608 | tf_op jit(solution)/shard_map/all_to_all | solution.py:265
  92.4 0.7 fusion.42
  93.1 1.6 %gather_fusion.3 = bf16[128,2,1024]{2,1,0:T(2,128)(2,1)S(1)} fusion(bf16[2,128,1024]{2,0,1:T(2,128)(2,1)S(1)} %get-tuple-element.14, s32[1024]{0:T(1024)S(1)} %pad_clamp_fusion), kind=kCustom, calls=%fused_computation.3.clone | custom fusion | bytes 1049088 | tf_op jit(solution)/shard_map/jit(_take)/gather | solution.py:259
  94.7 0.6 fusion.13
  95.3 1.0 fusion.4
  96.3 0.2 copy-done.1
  96.5 1.1 %add.131 = f32[2,4,32,1024]{3,2,1,0:T(8,128)} add(f32[2,4,32,1024]{3,2,1,0:T(8,128)S(1)} %copy-done.1, f32[2,4,32,1024]{3,2,1,0:T(8,128)S(1)} %bitcast.63) | non-fusion elementwise | flops 262144 | bytes 3145728 | tf_op jit(solution)/shard_map/add | solution.py:267
  97.6 1.6 %gather_fusion.2 = bf16[128,2,1024]{2,1,0:T(2,128)(2,1)S(1)} fusion(bf16[2,128,1024]{2,0,1:T(2,128)(2,1)S(1)} %get-tuple-element.15, s32[1024]{0:T(1024)S(1)} %pad_clamp_fusion.1), kind=kCustom, calls=%fused_computation.2.clone | custom fusion | bytes 1049088 | tf_op jit(solution)/shard_map/jit(_take)/gather | solution.py:259
  99.3 0.6 fusion.12
  99.9 1.0 fusion.1
  100.8 0.2 copy-done.2
  101.1 1.1 %add.128 = f32[2,4,32,1024]{3,2,1,0:T(8,128)} add(f32[2,4,32,1024]{3,2,1,0:T(8,128)S(1)} %copy-done.2, f32[2,4,32,1024]{3,2,1,0:T(8,128)S(1)} %bitcast.64) | non-fusion elementwise | flops 262144 | bytes 3145728 | tf_op jit(solution)/shard_map/add | solution.py:266
  (28 shorter events, 0.8 us)
Async XLA Ops:
  0.6 3.0 %copy-start.3 = (f32[2,4,1024]{2,1,0:T(4,128)S(1)}, f32[2,4,1024]{2,1,0:T(4,128)}, u32[]{:S(2)}) copy-start(f32[2,4,1024]{2,1,0:T(4,128)} %param.11) | copy-start | bytes 98308
  0.6 3.1 %copy-start = (f32[2,4,32,1024]{3,2,1,0:T(8,128)S(1)}, f32[2,4,32,1024]{3,2,1,0:T(8,128)}, u32[]{:S(2)}) copy-start(f32[2,4,32,1024]{3,2,1,0:T(8,128)} %vertex_ref.1) | copy-start | bytes 3145732
  64.7 27.7 %all-to-all-start = ((bf16[4,128,1024]{2,0,1:T(4,128)(2,1)}), bf16[4,128,1024]{2,0,1:T(4,128)(2,1)S(1)}, u32[]{:S(2)}, u32[]{:S(2)}) async-start(bf16[4,128,1024]{2,0,1:T(4,128)(2,1)} %pad_maximum_fusion), calls=%async_computation | async-start | bytes 2097152 | tf_op jit(solution)/shard_map/all_to_all | solution.py:265
  74.6 2.4 %copy-start.4 = (s32[2,1024]{1,0:T(2,128)S(1)}, s32[2,1024]{1,0:T(2,128)}, u32[]{:S(2)}) copy-start(s32[2,1024]{1,0:T(2,128)} %param.13) | copy-start | bytes 24580
  95.3 1.2 %copy-start.1 = (f32[2,4,32,1024]{3,2,1,0:T(8,128)S(1)}, f32[2,4,32,1024]{3,2,1,0:T(8,128)}, u32[]{:S(2)}) copy-start(f32[2,4,32,1024]{3,2,1,0:T(8,128)} %param.10) | copy-start | bytes 3145732
  99.8 1.2 %copy-start.2 = (f32[2,4,32,1024]{3,2,1,0:T(8,128)S(1)}, f32[2,4,32,1024]{3,2,1,0:T(8,128)}, u32[]{:S(2)}) copy-start(f32[2,4,32,1024]{3,2,1,0:T(8,128)} %param.9) | copy-start | bytes 3145732

commit v2 on v1

v2 whole, which is shorter than its diff:
```python
import jax
import jax.numpy as jnp
from jax import lax
from jax.experimental import pallas as pl
from jax.experimental.pallas import tpu as pltpu
from jax.sharding import PartitionSpec as P

LADDER = 6
MESH = pl.DeviceIdType.MESH
BF16 = jnp.bfloat16
F32 = jnp.float32
I32 = jnp.int32
K = 1024
ROWS = 32
QL = 4
MINE = 4 * ROWS
NB = 256
DEVS = 128
LANES = 128
TILE = 2 * K // LANES


def ladder_kernel(
    order_ref, vertex_ref, bubble_ref, col_ref, home_ref, crossed_ref,
    low, whole, base, full, left_op, outgoing, chi_own, chi, selector, sorted_rows, stage, packed,
    send1, send_chi, recv_chi, recv, send2, send3, send_home, recv_home,
    send_row, recv_row, own_row, known_half, known_all,
):
    pb, ka = lax.axis_index("pb"), lax.axis_index("ka")
    z_hi, core = pb // 2, pb % 2
    z_lo, y, x = ka // 16, (ka // 4) % 4, ka % 4
    line = ka - x
    me = pb * 32 + ka

    def taker(j):
        return (z_hi * 2 + 1 - z_lo, core * 16 + j * 4 + x)

    def giver(j):
        return (z_hi * 2 + z_lo, (1 - core) * 16 + j * 4 + x)

    right = (pb, line + (x + 1) % 4)
    left = (pb, line + (x + 3) % 4)
    partner = (z_hi * 2 + 1 - core, ka)
    across = (pb, (ka + 16) % 32)
    mirror = ((pb + 2) % 4, ka)

    barrier = pltpu.get_barrier_semaphore()
    for j in range(4):
        pl.semaphore_signal(barrier, inc=1, device_id=taker(j), device_id_type=MESH)
        pl.semaphore_signal(barrier, inc=1, device_id=giver(j), device_id_type=MESH)
    for other in (right, left, partner, across, mirror):
        pl.semaphore_signal(barrier, inc=1, device_id=other, device_id_type=MESH)
    for j in range(4):
        low[j] = vertex_ref[:, j].astype(BF16)
        chi_own[j] = bubble_ref[:, j]
    pl.semaphore_wait(barrier, 13)

    def rows_of(piece):
        return pl.ds(pl.multiple_of(piece * ROWS, ROWS), ROWS)

    def copy1(s):
        j = (y + s) % 4
        return pltpu.make_async_remote_copy(
            src_ref=low.at[j],
            dst_ref=whole.at[:, rows_of(ka), :],
            send_sem=send1.at[s],
            recv_sem=recv.at[ka],
            device_id=taker(j),
            device_id_type=MESH,
        )

    def chi_copy(s, slot):
        j = (y + s) % 4
        return pltpu.make_async_remote_copy(
            src_ref=chi_own.at[j],
            dst_ref=chi.at[slot],
            send_sem=send_chi.at[s],
            recv_sem=recv_chi.at[slot],
            device_id=taker(j),
            device_id_type=MESH,
        )

    def pass_on(piece, sem, target):
        block = whole.at[:, rows_of(piece), :]
        return pltpu.make_async_remote_copy(
            src_ref=block,
            dst_ref=block,
            send_sem=sem,
            recv_sem=recv.at[piece],
            device_id=target,
            device_id_type=MESH,
        )

    def piece_at(s, shift):
        return (1 - core) * 16 + (y + 4 - s) % 4 * 4 + (x + shift) % 4

    for s in range(4):
        copy1(s).start()
    for s in range(4):
        chi_copy(s, y).start()

    def select_rows(i, carry):
        at = pl.multiple_of(i * ROWS, ROWS)
        source = lax.broadcasted_iota(I32, (ROWS, K), 0) + at
        for c in range(2):
            hit = source == col_ref[c:c + 1, :]
            selector[c, pl.ds(at, ROWS), :] = jnp.where(hit, 1.0, 0.0).astype(BF16)
        return carry

    lax.fori_loop(0, K // ROWS, select_rows, 0)

    for s in range(4):
        piece = piece_at(s, 0)
        pass_on(piece, send2.at[s, 0], right).wait_recv()
        pass_on(piece, send2.at[s, 0], right).start()
        pass_on(piece, send2.at[s, 1], left).start()
        pass_on(piece, send3.at[s, 0], partner).start()
    for s in range(4):
        piece = piece_at(s, 3)
        pass_on(piece, send3.at[s, 1], partner).wait_recv()
        if s < 2:
            pass_on(piece, send2.at[s, 2], right).start()
        pass_on(piece, send3.at[s, 1], partner).start()
        piece = piece_at(s, 1)
        pass_on(piece, send3.at[s, 2], partner).wait_recv()
        if s >= 2:
            pass_on(piece, send2.at[s, 2], left).start()
        pass_on(piece, send3.at[s, 2], partner).start()
    for s in range(4):
        piece = piece_at(s, 2)
        pass_on(piece, send3.at[s, 3], partner).wait_recv()
        pass_on(piece, send3.at[s, 3], partner).start()

    for j in range(4):
        rows = whole[:, rows_of((1 - core) * 16 + j * 4 + x), :].astype(F32)
        base[:, j * ROWS:(j + 1) * ROWS, :] = rows
        full[:, j * ROWS:(j + 1) * ROWS, :] = rows
    for i in range(16):
        pass_on(core * 16 + i, send3.at[0, 0], partner).wait_recv()
    pl.semaphore_signal(known_half, inc=1, device_id=across, device_id_type=MESH)

    for s in range(4):
        chi_copy(s, s).wait_recv()
    chi_re = chi[0, 0:1, :]
    chi_im = chi[0, 1:2, :]

    def scale(i, carry):
        rows = pl.ds(pl.multiple_of(i * ROWS, ROWS), ROWS)
        re, im = full[0, rows, :], full[1, rows, :]
        left_op[rows, :] = (re * chi_re - im * chi_im).astype(BF16)
        low_rows = pl.ds(pl.multiple_of(MINE + i * ROWS, ROWS), ROWS)
        left_op[low_rows, :] = (re * chi_im + im * chi_re).astype(BF16)
        return carry

    def product(cols):
        by_re = jnp.dot(left_op[...], whole[0, :, cols], preferred_element_type=F32)
        by_im = jnp.dot(left_op[...], whole[1, :, cols], preferred_element_type=F32)
        return by_re[:MINE] - by_im[MINE:], by_im[:MINE] + by_re[MINE:]

    def step(_, carry):
        lax.fori_loop(0, MINE // ROWS, scale, 0)

        def columns(n, inner):
            cols = pl.ds(pl.multiple_of(n * NB, NB), NB)
            re, im = product(cols)
            full[0, :, cols] = base[0, :, cols] + re
            full[1, :, cols] = base[1, :, cols] + im
            return inner

        return lax.fori_loop(0, K // NB, columns, carry)

    lax.fori_loop(0, 2, step, 0)
    pl.semaphore_wait(known_half, 1)
    pl.semaphore_signal(known_all, inc=1, device_id=mirror, device_id_type=MESH)
    lax.fori_loop(0, LADDER - 3, step, 0)
    lax.fori_loop(0, MINE // ROWS, scale, 0)

    def last(n, carry):
        cols = pl.ds(pl.multiple_of(n * NB, NB), NB)
        re, im = product(cols)
        for j in range(4):
            outgoing[j, 0, :, cols] = re[j * ROWS:(j + 1) * ROWS].astype(BF16)
            outgoing[j, 1, :, cols] = im[j * ROWS:(j + 1) * ROWS].astype(BF16)
        return carry

    lax.fori_loop(0, K // NB, last, 0)

    def home_copy(s):
        j = (y + s) % 4
        return pltpu.make_async_remote_copy(
            src_ref=outgoing.at[j],
            dst_ref=home_ref.at[y],
            send_sem=send_home.at[s],
            recv_sem=recv_home.at[y],
            device_id=giver(j),
            device_id_type=MESH,
        )

    def from_home(j):
        return pltpu.make_async_remote_copy(
            src_ref=outgoing.at[j],
            dst_ref=home_ref.at[j],
            send_sem=send_home.at[j],
            recv_sem=recv_home.at[j],
            device_id=taker(j),
            device_id_type=MESH,
        )

    for s in range(4):
        home_copy(s).start()
    for s in range(4):
        copy1(s).wait_send()
        chi_copy(s, s).wait_send()
        for t in range(3):
            pass_on(piece_at(s, 0), send2.at[s, t], right).wait_send()
        for t in range(4):
            pass_on(piece_at(s, 0), send3.at[s, t], partner).wait_send()
    for j in range(4):
        from_home(j).wait_recv()
    pl.semaphore_wait(known_all, 1)

    def row_copy(c, target, slot):
        return pltpu.make_async_remote_copy(
            src_ref=packed.at[c, target],
            dst_ref=crossed_ref.at[c, slot],
            send_sem=send_row.at[c],
            recv_sem=recv_row.at[c],
            device_id=(target // 32, target % 32),
            device_id_type=MESH,
        )

    def own_copy(c):
        return pltpu.make_async_copy(packed.at[c, me], crossed_ref.at[c, me], own_row.at[c])

    for c in range(2):
        for p in range(2):
            rows = home_ref[:, p].reshape(MINE, K)
            sorted_rows[p * DEVS:(p + 1) * DEVS, :] = jnp.dot(
                order_ref[c], rows, preferred_element_type=F32
            ).astype(BF16)

        def cross_columns(n, carry):
            cols = pl.ds(pl.multiple_of(n * NB, NB), NB)
            moved = jnp.dot(sorted_rows[...], selector[c, :, cols], preferred_element_type=F32)
            for p in range(2):
                for h in range(NB // LANES):
                    start = p * (TILE // 2) + n * (NB // LANES) + h
                    stage[pl.ds(start, DEVS, stride=TILE), :] = moved[
                        p * DEVS:(p + 1) * DEVS, h * LANES:(h + 1) * LANES
                    ]
            return carry

        lax.fori_loop(0, K // NB, cross_columns, 0)

        def pack(t, carry):
            packed[c, t] = stage[pl.ds(pl.multiple_of(t * TILE, TILE), TILE), :].astype(BF16)
            return carry

        lax.fori_loop(0, DEVS, pack, 0, unroll=8)

        def send(i, carry):
            row_copy(c, (me + i) % DEVS, me).start()
            return carry

        lax.fori_loop(1, DEVS, send, 0)
        own_copy(c).start()

    for c in range(2):
        others = pltpu.make_async_remote_copy(
            src_ref=packed.at[c, pl.ds(0, DEVS - 1)],
            dst_ref=crossed_ref.at[c, pl.ds(0, DEVS - 1)],
            send_sem=send_row.at[c],
            recv_sem=recv_row.at[c],
            device_id=right,
            device_id_type=MESH,
        )
        others.wait_recv()
        others.wait_send()
        own_copy(c).wait()
    for s in range(4):
        home_copy(s).wait_send()


def run_ladder(order, vertex, bubble, col_maps):
    vmem = pl.BlockSpec(memory_space=pltpu.VMEM)
    return pl.pallas_call(
        ladder_kernel,
        out_shape=(
            jax.ShapeDtypeStruct((QL, 2, ROWS, K), BF16),
            jax.ShapeDtypeStruct((2, DEVS, TILE, LANES), BF16),
        ),
        in_specs=[vmem, vmem, vmem, vmem],
        out_specs=(vmem, pl.BlockSpec(memory_space=pl.ANY)),
        scratch_shapes=[
            pltpu.VMEM((QL, 2, ROWS, K), BF16),
            pltpu.VMEM((2, K, K), BF16),
            pltpu.VMEM((2, MINE, K), F32),
            pltpu.VMEM((2, MINE, K), F32),
            pltpu.VMEM((2 * MINE, K), BF16),
            pltpu.VMEM((QL, 2, ROWS, K), BF16),
            pltpu.VMEM((QL, 2, K), F32),
            pltpu.VMEM((QL, 2, K), F32),
            pltpu.VMEM((2, K, K), BF16),
            pltpu.VMEM((2 * DEVS, K), BF16),
            pltpu.VMEM((DEVS * TILE, LANES), F32),
            pltpu.VMEM((2, DEVS, TILE, LANES), BF16),
            pltpu.SemaphoreType.DMA((4,)),
            pltpu.SemaphoreType.DMA((4,)),
            pltpu.SemaphoreType.DMA((4,)),
            pltpu.SemaphoreType.DMA((32,)),
            pltpu.SemaphoreType.DMA((4, 3)),
            pltpu.SemaphoreType.DMA((4, 4)),
            pltpu.SemaphoreType.DMA((4,)),
            pltpu.SemaphoreType.DMA((4,)),
            pltpu.SemaphoreType.DMA((2,)),
            pltpu.SemaphoreType.DMA((2,)),
            pltpu.SemaphoreType.DMA((2,)),
            pltpu.SemaphoreType.REGULAR,
            pltpu.SemaphoreType.REGULAR,
        ],
        compiler_params=pltpu.CompilerParams(
            collective_id=0, has_side_effects=True, vmem_limit_bytes=44 * 2**20
        ),
    )(order, vertex, bubble, col_maps)


def finish_kernel(source_ref, home_ref, crossed_ref, vertex_ref, a_ref, b_ref, out_ref, out_a_ref, out_b_ref, stage):
    q = pl.program_id(0)
    for p in range(2):
        out_ref[p, 0] = vertex_ref[p, 0] + home_ref[0, p].astype(F32)
    for c, (add_ref, to_ref) in enumerate(((a_ref, out_a_ref), (b_ref, out_b_ref))):

        def place(r, carry):
            at = pl.multiple_of(r * TILE, TILE)
            stage[c, pl.ds(at, TILE), :] = crossed_ref[c, source_ref[c, q * ROWS + r]].astype(F32)
            return carry

        lax.fori_loop(0, ROWS, place, 0, unroll=8)
        for p in range(2):
            for h in range(K // LANES):
                cols = slice(h * LANES, (h + 1) * LANES)
                moved = stage[c, pl.ds(p * (TILE // 2) + h, ROWS, stride=TILE), :]
                to_ref[p, 0, :, cols] = add_ref[p, 0, :, cols] + moved


def finish(source, home, crossed, vertex, cross_a, cross_b):
    whole_block = pl.BlockSpec((2, DEVS, TILE, LANES), lambda q: (0, 0, 0, 0), pipeline_mode=pl.Buffered(1))
    row_block = pl.BlockSpec((2, 1, ROWS, K), lambda q: (0, q, 0, 0))
    shape = jax.ShapeDtypeStruct(vertex.shape, F32)
    return pl.pallas_call(
        finish_kernel,
        grid=(QL,),
        out_shape=(shape, shape, shape),
        in_specs=[
            pl.BlockSpec(memory_space=pltpu.SMEM),
            pl.BlockSpec((1, 2, ROWS, K), lambda q: (q, 0, 0, 0)),
            whole_block,
            row_block,
            row_block,
            row_block,
        ],
        out_specs=(row_block, row_block, row_block),
        scratch_shapes=[pltpu.VMEM((2, ROWS * TILE, LANES), F32)],
    )(source, home, crossed, vertex, cross_a, cross_b)


def per_device(vertex_ladder, vertex_cross_a, vertex_cross_b, bubble, row_maps, col_maps):
    q_local = vertex_ladder.shape[1]
    row_count = vertex_ladder.shape[2]
    col_count = vertex_ladder.shape[3]
    pb_count = lax.axis_size("pb")
    ka_count = lax.axis_size("ka")
    dev_count = pb_count * ka_count
    local_count = q_local * row_count
    pb, ka = lax.axis_index("pb"), lax.axis_index("ka")
    my_device = pb * ka_count + ka

    def device_of(rows):
        return rows // col_count // q_local * ka_count + rows % col_count // row_count

    by_device = (
        row_maps.reshape(2, pb_count, q_local, ka_count, row_count)
        .transpose(0, 1, 3, 2, 4)
        .reshape(2, dev_count, local_count)
    )
    local = by_device // col_count % q_local * row_count + by_device % row_count
    send_index = jnp.sum(jnp.where(device_of(by_device) == my_device, local, 0), 2)
    order = (send_index[:, :, None] == jnp.arange(local_count, dtype=I32)).astype(BF16)
    mine = lax.dynamic_slice(row_maps, (0, pb * q_local, ka * row_count), (2, q_local, row_count))
    source = device_of(mine).reshape(2, local_count)
    home, crossed = run_ladder(order, vertex_ladder, bubble, col_maps)
    return finish(source, home, crossed, vertex_ladder, vertex_cross_a, vertex_cross_b)


def solution(mesh):
    return jax.shard_map(
        per_device,
        mesh=mesh,
        in_specs=(
            P(None, "pb", "ka", None),
            P(None, "pb", "ka", None),
            P(None, "pb", "ka", None),
            P(None, "pb", None),
            P(),
            P(),
        ),
        out_specs=(P(None, "pb", "ka", None), P(None, "pb", "ka", None), P(None, "pb", "ka", None)),
        check_vma=False,
    )
```

time: 102 us -> 84.2 us (0.83)
  Pallas kernels: 53.9 us -> 76.5 us
  waiting for transfers between devices: 15.3 us -> 0 us
  starting transfers between devices: 8.59 us -> 0 us
  local copies, waits for them, and re-layouts: 12.3 us -> 4.24 us
  other arithmetic: 9.33 us -> 2.54 us
  matrix products: 1.97 us -> 0 us
    pallas_call x1 -> x2, Pallas kernels: 53.9 us -> 76.5 us  [the longest x1 71.1 us: run_ladder(): pl.pallas_call(ladder_kernel, out_shape=(jax.ShapeDtypeStruct((QL, 2, ROW...]
    all_to_all x1 -> x0, waiting for transfers between devices: 15.3 us -> none  [per_device(): lax.all_to_all(both, ('pb', 'ka'), split_axis=1, concat_axis=1, tiled=True)]
    all_to_all x1 -> x0, starting transfers between devices: 8.59 us -> none  [per_device(): lax.all_to_all(both, ('pb', 'ka'), split_axis=1, concat_axis=1, tiled=True)]
    gather x4 -> x0, local copies, waits for them, and re-layouts: 6.51 us -> none  [the longest x2 3.26 us: prepare(): return jnp.take(reducible, send_index, axis=1)]
    add x3 -> x1, other arithmetic: 3.32 us -> 0.88 us  [device_of(): rows // col_count // q_local * ka_count + rows % col_count // row_count]
    select_n x6 -> x0, other arithmetic: 2.3 us -> none  [the longest x4 1.15 us: prepare(): return jnp.take(reducible, send_index, axis=1)]
    concatenate x1 -> x0, other arithmetic: 2.05 us -> none  [per_device(): both = jnp.concatenate([prepare(row_maps[0]), prepare(row_maps[1])], axis=0)]
    dot_general x2 -> x0, matrix products: 1.97 us -> none  [place(): jnp.einsum('prk,km->prm', picked, selector, preferred_element_type=F32)]
  transfers between devices with their start and end apart: 1 -> 0, of which waited for: 1 -> 0; matrix products, arithmetic and copies ran while one was open for 4% -> 0% of each run, Pallas kernels for 0% -> 0%
where the time goes in v2:
time: 84.2 us; the launch traced here: 84 us
  Pallas kernels  76.5 us (91%)
  local copies, waits for them, and re-layouts  4.24 us (5%)
  other arithmetic  2.54 us (3%)
    pallas_call x1, Pallas kernels, run_ladder(): pl.pallas_call(ladder_kernel, out_shape=(jax.ShapeDtypeStruct((QL, 2, ROW...  71.1 us
    pallas_call x1, Pallas kernels, finish(): pl.pallas_call(finish_kernel, grid=(QL,), out_shape=(shape, shape, shape)...  5.4 us
    unnamed x10, local copies, waits for them, and re-layouts  2.42 us

profile of v2, /device:TPU:1, one launch (start us, length us, event | category | flops | bytes accessed | tf_op | source)
XLA Modules:
  0.0 84.0 jit_solution(775485803624927029)
XLA Ops:
  0.6 0.0 copy-start
  0.6 0.9 %fusion.16 = s32[2,4,32]{2,1,0:T(4,128)S(1)} fusion(s32[2,16,1024]{2,1,0:T(8,128)} %param.10, s32[]{:T(128)S(6)} %select_n.61, s32[]{:T(128)S(6)} %select_n.62), kind=kLoop, calls=%fused_computation.50 | loop fusion | flops 13056 | bytes 2056 | tf_op jit(solution)/shard_map/add | solution.py:379
  1.5 0.7 reshape.16.source_ref
  2.2 1.1 %reshape.17 = s32[2,4,4,32,32]{4,3,2,1,0:T(8,128)S(1)} reshape(s32[2,16,1024]{2,1,0:T(8,128)} %param.10) | data formatting | bytes 262144 | tf_op jit(solution)/shard_map/reshape | solution.py:382
  3.3 1.6 %fusion.7 = s32[2,4,32]{2,1,0:T(4,128)S(1)} fusion(s32[2,4,4,32,32]{4,3,2,1,0:T(8,128)S(1)} %reshape.17, s32[]{:T(128)S(6)} %add.58), kind=kLoop, calls=%fused_computation.23 | loop fusion | flops 2227968 | bytes 132100 | tf_op jit(solution)/shard_map/reduce_sum | solution.py:387
  4.8 0.1 eq.30
  4.9 0.0 copy-start.3
  4.9 0.0 copy-start.4
  4.9 0.1 fusion.13.order_ref
  5.0 0.0 copy-done
  5.0 0.6 copy-done.3
  5.7 0.0 copy-done.4
  5.7 71.1 %shard_map.85 = (bf16[4,2,32,1024]{3,2,1,0:T(8,128)(2,1)S(1)}, bf16[2,128,16,128]{3,2,1,0:T(8,128)(2,1)S(1)}) custom-call(bf16[2,128,128]{2,1,0:T(8,128)(2,1)S(1)} %fusion.13.order_ref, f32[2,4,32,1024]{3,2,1,0:T(8,128)S(1)} %copy-done, f32[2,4,1024]{2,1,0:T(4,128)S(1)} %copy-done.3, s32[2,1024]{1,0:T(2,128)S(1)} %copy-done.4), custom_call_target="tpu_custom_call" | custom-call | tf_op jit(solution)/shard_map/pallas_call | solution.py:286
  76.8 0.0 copy-start.1
  76.8 1.0 %copy-done.1 = bf16[2,128,16,128]{3,2,1,0:T(8,128)(2,1)} copy-done((bf16[2,128,16,128]{3,2,1,0:T(8,128)(2,1)}, bf16[2,128,16,128]{3,2,1,0:T(8,128)(2,1)S(1)}, u32[]{:S(2)}) %copy-start.1) | copy-done | bytes 1048600
  77.7 0.0 copy-start.2
  77.7 0.8 copy-done.2
  78.5 5.4 %shard_map.86 = (f32[2,4,32,1024]{3,2,1,0:T(8,128)}, f32[2,4,32,1024]{3,2,1,0:T(8,128)}, f32[2,4,32,1024]{3,2,1,0:T(8,128)}) custom-call(s32[2,128]{1,0:T(2,128)} %reshape.16.source_ref, bf16[4,2,32,1024]{3,2,1,0:T(8,128)(2,1)} %copy-done.2, bf16[2,128,16,128]{3,2,1,0:T(8,128)(2,1)} %copy-done.1, f32[2,4,32,1024]{3,2,1,0:T(8,128)} %vertex_ref.3, ...), custom_call_target="tpu_custom_call" | custom-call | tf_op jit(solution)/shard_map/pallas_call | solution.py:350
Async XLA Ops:
  0.6 4.4 %copy-start = (f32[2,4,32,1024]{3,2,1,0:T(8,128)S(1)}, f32[2,4,32,1024]{3,2,1,0:T(8,128)}, u32[]{:S(2)}) copy-start(f32[2,4,32,1024]{3,2,1,0:T(8,128)} %vertex_ref.3) | copy-start | bytes 3145732
  4.9 0.8 copy-start.3
  4.9 0.8 copy-start.4
  76.8 1.0 %copy-start.1 = (bf16[2,128,16,128]{3,2,1,0:T(8,128)(2,1)}, bf16[2,128,16,128]{3,2,1,0:T(8,128)(2,1)S(1)}, u32[]{:S(2)}) copy-start(bf16[2,128,16,128]{3,2,1,0:T(8,128)(2,1)S(1)} %get-tuple-element.6.crossed_ref) | copy-start | bytes 3145732
  77.7 0.8 copy-start.2

commit v3 on v2

v3 whole, which is shorter than its diff:
```python
import jax
import jax.numpy as jnp
from jax import lax
from jax.experimental import pallas as pl
from jax.experimental.pallas import tpu as pltpu
from jax.sharding import PartitionSpec as P

LADDER = 6
MESH = pl.DeviceIdType.MESH
BF16 = jnp.bfloat16
F32 = jnp.float32
I32 = jnp.int32
K = 1024
ROWS = 32
QL = 4
MINE = QL * ROWS
NB = 256
DEVS = 128
LANES = 128
HALF = K // 2
TILE = 16
BLOCKS = HALF // LANES
OVER_ROWS = (((0,), (0,)), ((), ()))


def one_hot(hit):
    return jnp.where(hit, 1.0, 0.0).astype(BF16)


def ladder_kernel(
    vertex_ref, bubble_ref, row_ref, col_ref, home_ref, to_a_ref, to_b_ref,
    vertex, low, whole, base, left_op, outgoing, home, chi_own, chi, selector, send_order, place_order,
    stage, packed, arrived, lined_up, placed,
    load, send1, send_chi, recv_chi, recv, send2, send3, send_home, recv_home,
    send_row, recv_row, own_row, known_half, known_all,
):
    pb, ka = lax.axis_index("pb"), lax.axis_index("ka")
    z_hi, core = pb // 2, pb % 2
    z_lo, y, x = ka // 16, (ka // 4) % 4, ka % 4
    line = ka - x
    me = pb * 32 + ka

    def taker(j):
        return (z_hi * 2 + 1 - z_lo, core * 16 + j * 4 + x)

    def giver(j):
        return (z_hi * 2 + z_lo, (1 - core) * 16 + j * 4 + x)

    right = (pb, line + (x + 1) % 4)
    left = (pb, line + (x + 3) % 4)
    partner = (z_hi * 2 + 1 - core, ka)
    across = (pb, (ka + 16) % 32)
    mirror = ((pb + 2) % 4, ka)

    vertex_copy = pltpu.make_async_copy(vertex_ref, vertex, load)
    vertex_copy.start()
    barrier = pltpu.get_barrier_semaphore()
    for j in range(4):
        pl.semaphore_signal(barrier, inc=1, device_id=taker(j), device_id_type=MESH)
        pl.semaphore_signal(barrier, inc=1, device_id=giver(j), device_id_type=MESH)
    for other in (right, left, partner, across, mirror):
        pl.semaphore_signal(barrier, inc=1, device_id=other, device_id_type=MESH)
    for j in range(QL):
        chi_own[j] = bubble_ref[:, j]
    vertex_copy.wait()
    for j in range(QL):
        low[j] = vertex[:, j].astype(BF16)
    pl.semaphore_wait(barrier, 13)

    def rows_of(piece):
        return pl.ds(pl.multiple_of(piece * ROWS, ROWS), ROWS)

    def copy1(s):
        j = (y + s) % 4
        return pltpu.make_async_remote_copy(
            src_ref=low.at[j],
            dst_ref=whole.at[:, rows_of(ka), :],
            send_sem=send1.at[s],
            recv_sem=recv.at[ka],
            device_id=taker(j),
            device_id_type=MESH,
        )

    def chi_copy(s, slot):
        j = (y + s) % 4
        return pltpu.make_async_remote_copy(
            src_ref=chi_own.at[j],
            dst_ref=chi.at[slot],
            send_sem=send_chi.at[s],
            recv_sem=recv_chi.at[slot],
            device_id=taker(j),
            device_id_type=MESH,
        )

    def pass_on(piece, sem, target):
        block = whole.at[:, rows_of(piece), :]
        return pltpu.make_async_remote_copy(
            src_ref=block,
            dst_ref=block,
            send_sem=sem,
            recv_sem=recv.at[piece],
            device_id=target,
            device_id_type=MESH,
        )

    def pass_plane(piece, plane, sem, target):
        block = whole.at[plane, rows_of(piece), :]
        return pltpu.make_async_remote_copy(
            src_ref=block,
            dst_ref=block,
            send_sem=sem,
            recv_sem=recv.at[piece],
            device_id=target,
            device_id_type=MESH,
        )

    def piece_at(s, shift):
        return (1 - core) * 16 + (y + 4 - s) % 4 * 4 + (x + shift) % 4

    for s in range(4):
        copy1(s).start()
    for s in range(4):
        chi_copy(s, y).start()

    for s in range(4):
        piece = piece_at(s, 0)
        pass_on(piece, send2.at[s, 0], right).wait_recv()
        pass_on(piece, send2.at[s, 0], right).start()
        pass_on(piece, send2.at[s, 1], left).start()
        pass_on(piece, send3.at[s, 0], partner).start()

    def select_rows(i, carry):
        at = pl.multiple_of(i * ROWS, ROWS)
        source = lax.broadcasted_iota(I32, (ROWS, K), 0) + at
        for c in range(2):
            selector[c, pl.ds(at, ROWS), :] = one_hot(source == col_ref[c:c + 1, :])
        return carry

    lax.fori_loop(0, K // ROWS, select_rows, 0)
    at_row = lax.broadcasted_iota(I32, (K, LANES), 0)
    at_lane = lax.broadcasted_iota(I32, (K, LANES), 1)
    by_ka = one_hot((at_lane % 32) == (at_row // 32))
    by_own = one_hot(((at_lane % 32) == (at_row % 32)) & ((at_row // 32) == ka))
    table_row = lax.broadcasted_iota(I32, (16, LANES), 0)
    table_lane = lax.broadcasted_iota(I32, (16, LANES), 1)
    for c in range(2):
        table = row_ref[c]
        owner = table // (QL * K) * 32 + table % K // ROWS
        local = table // K % QL * ROWS + table % ROWS
        wanted = jnp.where(owner == me, local + 1, 0).astype(F32).astype(BF16)
        wanted = jnp.dot(wanted, by_ka, preferred_element_type=F32)
        wanted = jnp.where(table_row // QL == table_lane // 32, wanted, 0.0)
        wanted = jnp.sum(wanted, axis=0, keepdims=True)
        local_row = (lax.broadcasted_iota(I32, (MINE, DEVS), 0) + 1).astype(F32)
        send_order[:, c * DEVS:(c + 1) * DEVS] = one_hot(local_row == wanted)
        owner = jnp.dot(owner.astype(F32).astype(BF16), by_own, preferred_element_type=F32)
        owner = jnp.where(table_row == pb * QL + table_lane // 32, owner, 0.0)
        owner = jnp.sum(owner, axis=0, keepdims=True)
        device = lax.broadcasted_iota(I32, (DEVS, MINE), 0).astype(F32)
        place_order[c] = one_hot(device == owner)

    for s in range(4):
        piece = piece_at(s, 3)
        pass_on(piece, send3.at[s, 1], partner).wait_recv()
        pass_plane(piece, 0, send2.at[s, 2], right).start()
        pass_on(piece, send3.at[s, 1], partner).start()
        piece = piece_at(s, 1)
        pass_on(piece, send3.at[s, 2], partner).wait_recv()
        pass_plane(piece, 1, send2.at[s, 3], left).start()
        pass_on(piece, send3.at[s, 2], partner).start()

    for s in range(4):
        chi_copy(s, s).wait_recv()

    def scaled(re, im, cols):
        chi_re, chi_im = chi[0, 0:1, cols], chi[0, 1:2, cols]
        return (re * chi_re - im * chi_im).astype(BF16), (re * chi_im + im * chi_re).astype(BF16)

    for j in range(4):
        at = j * ROWS
        rows = whole[:, rows_of((1 - core) * 16 + j * 4 + x), :].astype(F32)
        base[:, at:at + ROWS, :] = rows
        left_op[0, at:at + ROWS, :], left_op[0, MINE + at:MINE + at + ROWS, :] = scaled(rows[0], rows[1], slice(0, K))

    for s in range(4):
        piece = piece_at(s, 2)
        pass_on(piece, send3.at[s, 3], partner).wait_recv()
        pass_on(piece, send3.at[s, 3], partner).start()
    for i in range(16):
        pass_on(core * 16 + i, send3.at[0, 0], partner).wait_recv()
    pl.semaphore_signal(known_half, inc=1, device_id=across, device_id_type=MESH)

    def product(now, n):
        cols = slice(n * NB, (n + 1) * NB)
        by_re = jnp.dot(left_op[now], whole[0, :, cols], preferred_element_type=F32)
        by_im = jnp.dot(left_op[now], whole[1, :, cols], preferred_element_type=F32)
        return by_re[:MINE] - by_im[MINE:], by_im[:MINE] + by_re[MINE:]

    def step(i, carry):
        now = i % 2
        for n in range(K // NB):
            cols = slice(n * NB, (n + 1) * NB)
            re, im = product(now, n)
            re, im = scaled(base[0, :, cols] + re, base[1, :, cols] + im, cols)
            left_op[1 - now, 0:MINE, cols] = re
            left_op[1 - now, MINE:2 * MINE, cols] = im
        return carry

    lax.fori_loop(0, 2, step, 0)
    pl.semaphore_wait(known_half, 1)
    pl.semaphore_signal(known_all, inc=1, device_id=mirror, device_id_type=MESH)
    lax.fori_loop(2, LADDER - 1, step, 0)

    def home_copy(h, s):
        j = (y + s) % 4
        return pltpu.make_async_remote_copy(
            src_ref=outgoing.at[h, j],
            dst_ref=home.at[h, y],
            send_sem=send_home.at[h, s],
            recv_sem=recv_home.at[h, y],
            device_id=giver(j),
            device_id_type=MESH,
        )

    def from_home(h, j):
        return pltpu.make_async_remote_copy(
            src_ref=outgoing.at[h, j],
            dst_ref=home.at[h, j],
            send_sem=send_home.at[h, j],
            recv_sem=recv_home.at[h, j],
            device_id=taker(j),
            device_id_type=MESH,
        )

    for n in range(K // NB):
        re, im = product((LADDER - 1) % 2, n)
        h = n * NB // HALF
        cols = slice(n * NB % HALF, n * NB % HALF + NB)
        for j in range(4):
            outgoing[h, j, 0, :, cols] = re[j * ROWS:(j + 1) * ROWS].astype(BF16)
            outgoing[h, j, 1, :, cols] = im[j * ROWS:(j + 1) * ROWS].astype(BF16)
        if (n + 1) * NB % HALF == 0:
            for s in range(4):
                home_copy(h, s).start()

    for s in range(4):
        copy1(s).wait_send()
        chi_copy(s, s).wait_send()
        for t in range(2):
            pass_on(piece_at(s, 0), send2.at[s, t], right).wait_send()
        for t in range(2, 4):
            pass_plane(piece_at(s, 0), 0, send2.at[s, t], right).wait_send()
        for t in range(4):
            pass_on(piece_at(s, 0), send3.at[s, t], partner).wait_send()

    def row_copy(h, target):
        return pltpu.make_async_remote_copy(
            src_ref=packed.at[h, target],
            dst_ref=arrived.at[h, me],
            send_sem=send_row.at[h],
            recv_sem=recv_row.at[h],
            device_id=(target // 32, target % 32),
            device_id_type=MESH,
        )

    def own_copy(h):
        return pltpu.make_async_copy(packed.at[h, me], arrived.at[h, me], own_row.at[h])

    def others(h):
        return pltpu.make_async_remote_copy(
            src_ref=packed.at[h, pl.ds(0, DEVS - 1)],
            dst_ref=arrived.at[h, pl.ds(0, DEVS - 1)],
            send_sem=send_row.at[h],
            recv_sem=recv_row.at[h],
            device_id=right,
            device_id_type=MESH,
        )

    for h in range(2):
        for s in range(4):
            from_home(h, s).wait_recv()
        if h == 0:
            pl.semaphore_wait(known_all, 1)
        for p in range(2):
            rows = home[h, :, p].reshape(MINE, HALF)
            ordered = lax.dot_general(send_order[...], rows, OVER_ROWS, preferred_element_type=F32)
            for c in range(2):
                for b in range(BLOCKS):
                    stage[pl.ds((c * 2 + p) * BLOCKS + b, DEVS, stride=TILE), :] = ordered[
                        c * DEVS:(c + 1) * DEVS, b * LANES:(b + 1) * LANES
                    ]

        def pack(t, carry):
            packed[h, t] = stage[pl.ds(pl.multiple_of(t * TILE, TILE), TILE), :].astype(BF16)
            return carry

        lax.fori_loop(0, DEVS, pack, 0, unroll=8)

        def send(i, carry):
            row_copy(h, (me + i) % DEVS).start()
            return carry

        lax.fori_loop(1, DEVS, send, 0)
        own_copy(h).start()

    for h in range(2):
        for p in range(2):
            for q in range(QL):
                home_ref[p, q, :, h * HALF:(h + 1) * HALF] = home[h, q, p]

    for h in range(2):
        others(h).wait_recv()
        own_copy(h).wait()

        def unpack(t, carry):
            stage[pl.ds(pl.multiple_of(t * TILE, TILE), TILE), :] = arrived[h, t].astype(F32)
            return carry

        lax.fori_loop(0, DEVS, unpack, 0, unroll=8)
        for b in range(4 * BLOCKS):
            lined_up[:, b * LANES:(b + 1) * LANES] = stage[pl.ds(b, DEVS, stride=TILE), :].astype(BF16)
        for c, to_ref in enumerate((to_a_ref, to_b_ref)):
            for p in range(2):
                rows = lined_up[:, (c * 2 + p) * HALF:(c * 2 + p + 1) * HALF]
                placed[p * MINE:(p + 1) * MINE, :] = lax.dot_general(
                    place_order[c], rows, OVER_ROWS, preferred_element_type=F32
                ).astype(BF16)
            for n in range(K // NB):
                cols = slice(n * NB, (n + 1) * NB)
                moved = jnp.dot(
                    placed[...], selector[c, h * HALF:(h + 1) * HALF, cols], preferred_element_type=F32
                )
                moved = moved.reshape(2, QL, ROWS, NB)
                if h == 0:
                    to_ref[:, :, :, cols] = moved.astype(BF16)
                else:
                    to_ref[:, :, :, cols] = (to_ref[:, :, :, cols].astype(F32) + moved).astype(BF16)

    for h in range(2):
        others(h).wait_send()
        for s in range(4):
            home_copy(h, s).wait_send()


def run_ladder(vertex, bubble, row_maps, col_maps):
    vmem = pl.BlockSpec(memory_space=pltpu.VMEM)
    out = jax.ShapeDtypeStruct((2, QL, ROWS, K), BF16)
    return pl.pallas_call(
        ladder_kernel,
        out_shape=(out, out, out),
        in_specs=[pl.BlockSpec(memory_space=pl.ANY), vmem, vmem, vmem],
        out_specs=(vmem, vmem, vmem),
        scratch_shapes=[
            pltpu.VMEM((2, QL, ROWS, K), F32),
            pltpu.VMEM((QL, 2, ROWS, K), BF16),
            pltpu.VMEM((2, K, K), BF16),
            pltpu.VMEM((2, MINE, K), F32),
            pltpu.VMEM((2, 2 * MINE, K), BF16),
            pltpu.VMEM((2, QL, 2, ROWS, HALF), BF16),
            pltpu.VMEM((2, QL, 2, ROWS, HALF), BF16),
            pltpu.VMEM((QL, 2, K), F32),
            pltpu.VMEM((QL, 2, K), F32),
            pltpu.VMEM((2, K, K), BF16),
            pltpu.VMEM((MINE, 2 * DEVS), BF16),
            pltpu.VMEM((2, DEVS, MINE), BF16),
            pltpu.VMEM((DEVS * TILE, LANES), F32),
            pltpu.VMEM((2, DEVS, TILE, LANES), BF16),
            pltpu.VMEM((2, DEVS, TILE, LANES), BF16),
            pltpu.VMEM((DEVS, 4 * HALF), BF16),
            pltpu.VMEM((2 * MINE, HALF), BF16),
            pltpu.SemaphoreType.DMA,
            pltpu.SemaphoreType.DMA((4,)),
            pltpu.SemaphoreType.DMA((4,)),
            pltpu.SemaphoreType.DMA((4,)),
            pltpu.SemaphoreType.DMA((32,)),
            pltpu.SemaphoreType.DMA((4, 4)),
            pltpu.SemaphoreType.DMA((4, 4)),
            pltpu.SemaphoreType.DMA((2, 4)),
            pltpu.SemaphoreType.DMA((2, 4)),
            pltpu.SemaphoreType.DMA((2,)),
            pltpu.SemaphoreType.DMA((2,)),
            pltpu.SemaphoreType.DMA((2,)),
            pltpu.SemaphoreType.REGULAR,
            pltpu.SemaphoreType.REGULAR,
        ],
        compiler_params=pltpu.CompilerParams(
            collective_id=0, has_side_effects=True, vmem_limit_bytes=56 * 2**20
        ),
    )(vertex, bubble, row_maps, col_maps)


def per_device(vertex_ladder, vertex_cross_a, vertex_cross_b, bubble, row_maps, col_maps):
    home, to_a, to_b = run_ladder(vertex_ladder, bubble, row_maps, col_maps)
    return (
        vertex_ladder + home.astype(F32),
        vertex_cross_a + to_a.astype(F32),
        vertex_cross_b + to_b.astype(F32),
    )


def solution(mesh):
    return jax.shard_map(
        per_device,
        mesh=mesh,
        in_specs=(
            P(None, "pb", "ka", None),
            P(None, "pb", "ka", None),
            P(None, "pb", "ka", None),
            P(None, "pb", None),
            P(),
            P(),
        ),
        out_specs=(P(None, "pb", "ka", None), P(None, "pb", "ka", None), P(None, "pb", "ka", None)),
        check_vma=False,
    )
```

time: 84.2 us -> 76.8 us (0.912)
  Pallas kernels: 76.5 us -> 71.2 us
  local copies, waits for them, and re-layouts: 4.24 us -> 0.01 us
  other arithmetic: 2.54 us -> 4.52 us
    pallas_call x2 -> x1, Pallas kernels: 76.5 us -> 71.2 us  [run_ladder(): pl.pallas_call(ladder_kernel, out_shape=(out, out, out), in_specs=[pl.Blo...]
    add x1 -> x2, other arithmetic: 0.88 us -> 4.52 us  [the longest x1 3.41 us: per_device(): vertex_cross_b + to_b.astype(F32)]
    unnamed x10 -> x6, local copies, waits for them, and re-layouts: 2.42 us -> 0.01 us
    reshape x2 -> x0, local copies, waits for them, and re-layouts: 1.74 us -> none  [the longest x1 1.07 us: per_device(): row_maps.reshape(2, pb_count, q_local, ka_count, row_count)]
    reduce_sum x1 -> x0, other arithmetic: 1.55 us -> none  [per_device(): jnp.sum(jnp.where(device_of(by_device) == my_device, local, 0), 2)]
where the time goes in v3:
time: 76.8 us; the launch traced here: 76.4 us
  Pallas kernels  71.2 us (93%)
  other arithmetic  4.52 us (6%)
    pallas_call x1, Pallas kernels, run_ladder(): pl.pallas_call(ladder_kernel, out_shape=(out, out, out), in_specs=[pl.Blo...  71.2 us
    add x1, other arithmetic, per_device(): vertex_cross_b + to_b.astype(F32)  3.41 us

profile of v3, /device:TPU:1, one launch (start us, length us, event | category | flops | bytes accessed | tf_op | source)
XLA Modules:
  0.0 76.4 jit_solution(7031500471549475428)
XLA Ops:
  0.6 0.0 copy-start.1
  0.6 71.2 %shard_map.85 = (bf16[2,4,32,1024]{3,2,1,0:T(8,128)(2,1)}, bf16[2,4,32,1024]{3,2,1,0:T(8,128)(2,1)}, bf16[2,4,32,1024]{3,2,1,0:T(8,128)(2,1)}) custom-call(f32[2,4,32,1024]{3,2,1,0:T(8,128)} %vertex_ref.1, f32[2,4,1024]{2,1,0:T(4,128)} %bubble_ref.1, s32[2,16,1024]{2,1,0:T(8,128)} %row_ref.1, s32[2,1024]{1,0:T(2,128)} %col_ref.1), custom_call_target="tpu_custom_call" | custom-call | tf_op jit(solution)/shard_map/pallas_call | solution.py:348
  71.9 0.0 copy-done.1
  71.9 0.0 copy-start
  71.9 0.0 copy-start.2
  71.9 3.4 %convert_add_fusion = (f32[2,4,32,1024]{3,2,1,0:T(8,128)}, f32[2,4,32,1024]{3,2,1,0:T(8,128)}) fusion(f32[2,4,32,1024]{3,2,1,0:T(8,128)S(1)} %copy-done.1, bf16[2,4,32,1024]{3,2,1,0:T(8,128)(2,1)} %get-tuple-element.8, f32[2,4,32,1024]{3,2,1,0:T(8,128)} %param.7, bf16[2,4,32,1024]{3,2,1,0:T(8,128)(2,1)} %get-tuple-element.7), kind=kLoop, calls=%fused_computation | loop fusion | flops 1048576 | bytes 5242880 | tf_op jit(solution)/shard_map/add | solution.py:397
  75.3 0.0 copy-done
  75.3 0.0 copy-done.2
  75.3 1.1 %convert_add_fusion.2 = f32[2,4,32,1024]{3,2,1,0:T(8,128)} fusion(f32[2,4,32,1024]{3,2,1,0:T(8,128)S(1)} %copy-done, bf16[2,4,32,1024]{3,2,1,0:T(8,128)(2,1)S(1)} %copy-done.2), kind=kLoop, calls=%fused_computation.2 | loop fusion | flops 524288 | bytes 2621440 | tf_op jit(solution)/shard_map/add | solution.py:395
Async XLA Ops:
  0.6 71.2 %copy-start.1 = (f32[2,4,32,1024]{3,2,1,0:T(8,128)S(1)}, f32[2,4,32,1024]{3,2,1,0:T(8,128)}, u32[]{:S(2)}) copy-start(f32[2,4,32,1024]{3,2,1,0:T(8,128)} %param.8) | copy-start | bytes 3145732
  71.9 3.4 %copy-start = (f32[2,4,32,1024]{3,2,1,0:T(8,128)S(1)}, f32[2,4,32,1024]{3,2,1,0:T(8,128)}, u32[]{:S(2)}) copy-start(f32[2,4,32,1024]{3,2,1,0:T(8,128)} %vertex_ref.1) | copy-start | bytes 3145732
  71.9 3.4 %copy-start.2 = (bf16[2,4,32,1024]{3,2,1,0:T(8,128)(2,1)S(1)}, bf16[2,4,32,1024]{3,2,1,0:T(8,128)(2,1)}, u32[]{:S(2)}) copy-start(bf16[2,4,32,1024]{3,2,1,0:T(8,128)(2,1)} %get-tuple-element.6) | copy-start | bytes 1572868

commit v4 on v3

--- a/solution.py
+++ b/solution.py
@@ -29,7 +29,7 @@
 
 def ladder_kernel(
     vertex_ref, bubble_ref, row_ref, col_ref, home_ref, to_a_ref, to_b_ref,
-    vertex, low, whole, base, left_op, outgoing, home, chi_own, chi, selector, send_order, place_order,
+    vertex, low, whole, base, left_even, left_odd, outgoing, home, chi_own, chi, selector, send_order, place_order,
     stage, packed, arrived, lined_up, placed,
     load, send1, send_chi, recv_chi, recv, send2, send3, send_home, recv_home,
     send_row, recv_row, own_row, known_half, known_all,
@@ -178,9 +178,11 @@
 
     for j in range(4):
         at = j * ROWS
-        rows = whole[:, rows_of((1 - core) * 16 + j * 4 + x), :].astype(F32)
+        rows = whole[:, rows_of((1 - core) * 16 + j * 4 + x), :]
         base[:, at:at + ROWS, :] = rows
-        left_op[0, at:at + ROWS, :], left_op[0, MINE + at:MINE + at + ROWS, :] = scaled(rows[0], rows[1], slice(0, K))
+        re, im = scaled(rows[0].astype(F32), rows[1].astype(F32), slice(0, K))
+        left_even[at:at + ROWS, :] = re
+        left_even[MINE + at:MINE + at + ROWS, :] = im
 
     for s in range(4):
         piece = piece_at(s, 2)
@@ -190,26 +192,33 @@
         pass_on(core * 16 + i, send3.at[0, 0], partner).wait_recv()
     pl.semaphore_signal(known_half, inc=1, device_id=across, device_id_type=MESH)
 
-    def product(now, n):
+    def product(left_op, n):
         cols = slice(n * NB, (n + 1) * NB)
-        by_re = jnp.dot(left_op[now], whole[0, :, cols], preferred_element_type=F32)
-        by_im = jnp.dot(left_op[now], whole[1, :, cols], preferred_element_type=F32)
+        by_re = jnp.dot(left_op[...], whole[0, :, cols], preferred_element_type=F32)
+        by_im = jnp.dot(left_op[...], whole[1, :, cols], preferred_element_type=F32)
         return by_re[:MINE] - by_im[MINE:], by_im[:MINE] + by_re[MINE:]
 
-    def step(i, carry):
-        now = i % 2
+    def step(now, later):
         for n in range(K // NB):
             cols = slice(n * NB, (n + 1) * NB)
             re, im = product(now, n)
-            re, im = scaled(base[0, :, cols] + re, base[1, :, cols] + im, cols)
-            left_op[1 - now, 0:MINE, cols] = re
-            left_op[1 - now, MINE:2 * MINE, cols] = im
+            re, im = scaled(base[0, :, cols].astype(F32) + re, base[1, :, cols].astype(F32) + im, cols)
+            later[0:MINE, cols] = re
+            later[MINE:2 * MINE, cols] = im
+
+    def two_steps(i, carry):
+        step(left_even, left_odd)
+        step(left_odd, left_even)
+
+        @pl.when(i == 0)
+        def _():
+            pl.semaphore_wait(known_half, 1)
+            pl.semaphore_signal(known_all, inc=1, device_id=mirror, device_id_type=MESH)
+
         return carry
 
-    lax.fori_loop(0, 2, step, 0)
-    pl.semaphore_wait(known_half, 1)
-    pl.semaphore_signal(known_all, inc=1, device_id=mirror, device_id_type=MESH)
-    lax.fori_loop(2, LADDER - 1, step, 0)
+    lax.fori_loop(0, LADDER // 2 - 1, two_steps, 0)
+    step(left_even, left_odd)
 
     def home_copy(h, s):
         j = (y + s) % 4
@@ -233,7 +242,7 @@
         )
 
     for n in range(K // NB):
-        re, im = product((LADDER - 1) % 2, n)
+        re, im = product(left_odd, n)
         h = n * NB // HALF
         cols = slice(n * NB % HALF, n * NB % HALF + NB)
         for j in range(4):
@@ -354,8 +363,9 @@
             pltpu.VMEM((2, QL, ROWS, K), F32),
             pltpu.VMEM((QL, 2, ROWS, K), BF16),
             pltpu.VMEM((2, K, K), BF16),
-            pltpu.VMEM((2, MINE, K), F32),
-            pltpu.VMEM((2, 2 * MINE, K), BF16),
+            pltpu.VMEM((2, MINE, K), BF16),
+            pltpu.VMEM((2 * MINE, K), BF16),
+            pltpu.VMEM((2 * MINE, K), BF16),
             pltpu.VMEM((2, QL, 2, ROWS, HALF), BF16),
             pltpu.VMEM((2, QL, 2, ROWS, HALF), BF16),
             pltpu.VMEM((QL, 2, K), F32),
@@ -384,7 +394,7 @@
             pltpu.SemaphoreType.REGULAR,
         ],
         compiler_params=pltpu.CompilerParams(
-            collective_id=0, has_side_effects=True, vmem_limit_bytes=56 * 2**20
+            collective_id=0, has_side_effects=True, vmem_limit_bytes=28 * 2**20
         ),
     )(vertex, bubble, row_maps, col_maps)
 

time: 76.8 us -> 71.6 us (0.932)
  Pallas kernels: 71.2 us -> 63 us
  local copies, waits for them, and re-layouts: 0.01 us -> 3.58 us
    pallas_call x1, Pallas kernels: 71.2 us -> 63 us  [run_ladder(): pl.pallas_call(ladder_kernel, out_shape=(out, out, out), in_specs=[pl.Blo...]
    unnamed x6 -> x10, local copies, waits for them, and re-layouts: 0.01 us -> 3.58 us
where the time goes in v4:
time: 71.6 us; the launch traced here: 71.3 us
  Pallas kernels  63 us (88%)
  other arithmetic  4.09 us (6%)
  local copies, waits for them, and re-layouts  3.58 us (5%)
    pallas_call x1, Pallas kernels, run_ladder(): pl.pallas_call(ladder_kernel, out_shape=(out, out, out), in_specs=[pl.Blo...  63 us
    unnamed x10, local copies, waits for them, and re-layouts  3.58 us
    add x1, other arithmetic, per_device(): vertex_cross_b + to_b.astype(F32)  2.93 us

profile of v4, /device:TPU:1, one launch (start us, length us, event | category | flops | bytes accessed | tf_op | source)
XLA Modules:
  0.0 71.3 jit_solution(11670507378004682811)
XLA Ops:
  0.6 0.0 copy-start
  0.6 1.2 %copy-done = f32[2,4,32,1024]{3,2,1,0:T(8,128)S(1)} copy-done((f32[2,4,32,1024]{3,2,1,0:T(8,128)S(1)}, f32[2,4,32,1024]{3,2,1,0:T(8,128)}, u32[]{:S(2)}) %copy-start) | copy-done | bytes 1048600
  1.9 0.0 copy-start.1
  1.9 0.9 %copy-done.1 = s32[2,16,1024]{2,1,0:T(8,128)S(1)} copy-done((s32[2,16,1024]{2,1,0:T(8,128)S(1)}, s32[2,16,1024]{2,1,0:T(8,128)}, u32[]{:S(2)}) %copy-start.1) | copy-done | bytes 131096
  2.8 0.0 copy-start.2
  2.8 0.8 %copy-done.2 = f32[2,4,1024]{2,1,0:T(4,128)S(1)} copy-done((f32[2,4,1024]{2,1,0:T(4,128)S(1)}, f32[2,4,1024]{2,1,0:T(4,128)}, u32[]{:S(2)}) %copy-start.2) | copy-done | bytes 32792
  3.5 0.0 copy-start.3
  3.5 0.7 copy-done.3
  4.2 0.0 copy-start.4
  4.2 63.0 %shard_map.85 = (bf16[2,4,32,1024]{3,2,1,0:T(8,128)(2,1)S(1)}, bf16[2,4,32,1024]{3,2,1,0:T(8,128)(2,1)S(1)}, bf16[2,4,32,1024]{3,2,1,0:T(8,128)(2,1)S(1)}) custom-call(f32[2,4,32,1024]{3,2,1,0:T(8,128)S(1)} %copy-done, f32[2,4,1024]{2,1,0:T(4,128)S(1)} %copy-done.2, s32[2,16,1024]{2,1,0:T(8,128)S(1)} %copy-done.1, s32[2,1024]{1,0:T(2,128)S(1)} %copy-done.3), custom_call_target="tpu_custom_call" | custom-call | tf_op jit(solution)/shard_map/pallas_call | solution.py:357
  67.2 0.0 copy-done.4
  67.2 2.9 %convert_add_fusion = (f32[2,4,32,1024]{3,2,1,0:T(8,128)}, f32[2,4,32,1024]{3,2,1,0:T(8,128)}) fusion(f32[2,4,32,1024]{3,2,1,0:T(8,128)S(1)} %copy-done.4, bf16[2,4,32,1024]{3,2,1,0:T(8,128)(2,1)S(1)} %get-tuple-element.8, f32[2,4,32,1024]{3,2,1,0:T(8,128)} %param.7, bf16[2,4,32,1024]{3,2,1,0:T(8,128)(2,1)S(1)} %get-tuple-element.7), kind=kLoop, calls=%fused_computation | loop fusion | flops 1048576 | bytes 5242880 | tf_op jit(solution)/shard_map/add | solution.py:407
  70.2 1.2 %convert_add_fusion.2 = f32[2,4,32,1024]{3,2,1,0:T(8,128)} fusion(f32[2,4,32,1024]{3,2,1,0:T(8,128)S(1)} %copy-done, bf16[2,4,32,1024]{3,2,1,0:T(8,128)(2,1)S(1)} %get-tuple-element.6), kind=kLoop, calls=%fused_computation.2 | loop fusion | flops 524288 | bytes 2621440 | tf_op jit(solution)/shard_map/add | solution.py:405
Async XLA Ops:
  0.6 1.2 %copy-start = (f32[2,4,32,1024]{3,2,1,0:T(8,128)S(1)}, f32[2,4,32,1024]{3,2,1,0:T(8,128)}, u32[]{:S(2)}) copy-start(f32[2,4,32,1024]{3,2,1,0:T(8,128)} %vertex_ref.1) | copy-start | bytes 3145732
  1.9 0.9 %copy-start.1 = (s32[2,16,1024]{2,1,0:T(8,128)S(1)}, s32[2,16,1024]{2,1,0:T(8,128)}, u32[]{:S(2)}) copy-start(s32[2,16,1024]{2,1,0:T(8,128)} %row_ref.1) | copy-start | bytes 393220
  2.8 0.8 %copy-start.2 = (f32[2,4,1024]{2,1,0:T(4,128)S(1)}, f32[2,4,1024]{2,1,0:T(4,128)}, u32[]{:S(2)}) copy-start(f32[2,4,1024]{2,1,0:T(4,128)} %bubble_ref.1) | copy-start | bytes 98308
  3.5 0.7 copy-start.3
  4.2 63.0 %copy-start.4 = (f32[2,4,32,1024]{3,2,1,0:T(8,128)S(1)}, f32[2,4,32,1024]{3,2,1,0:T(8,128)}, u32[]{:S(2)}) copy-start(f32[2,4,32,1024]{3,2,1,0:T(8,128)} %param.8) | copy-start | bytes 3145732

commit v5 on v4

--- a/solution.py
+++ b/solution.py
@@ -28,10 +28,10 @@
 
 
 def ladder_kernel(
-    vertex_ref, bubble_ref, row_ref, col_ref, home_ref, to_a_ref, to_b_ref,
-    vertex, low, whole, base, left_even, left_odd, outgoing, home, chi_own, chi, selector, send_order, place_order,
+    vertex_ref, a_ref, b_ref, bubble_ref, row_ref, col_ref, to_ref, to_a_ref, to_b_ref,
+    out_ref, out_a_ref, out_b_ref, bubble, rows_from, cols_from, low, whole, base, left_even, left_odd, outgoing, home, chi_own, chi, selector, send_order, place_order,
     stage, packed, arrived, lined_up, placed,
-    load, send1, send_chi, recv_chi, recv, send2, send3, send_home, recv_home,
+    load, store, send1, send_chi, recv_chi, recv, send2, send3, send_home, recv_home,
     send_row, recv_row, own_row, known_half, known_all,
 ):
     pb, ka = lax.axis_index("pb"), lax.axis_index("ka")
@@ -52,19 +52,27 @@
     across = (pb, (ka + 16) % 32)
     mirror = ((pb + 2) % 4, ka)
 
-    vertex_copy = pltpu.make_async_copy(vertex_ref, vertex, load)
-    vertex_copy.start()
+    loads = [
+        pltpu.make_async_copy(source, target, load.at[i])
+        for i, (source, target) in enumerate((
+            (vertex_ref, out_ref), (bubble_ref, bubble), (row_ref, rows_from), (col_ref, cols_from),
+            (a_ref, out_a_ref), (b_ref, out_b_ref),
+        ))
+    ]
+    loads[0].start()
+    loads[1].start()
     barrier = pltpu.get_barrier_semaphore()
     for j in range(4):
         pl.semaphore_signal(barrier, inc=1, device_id=taker(j), device_id_type=MESH)
         pl.semaphore_signal(barrier, inc=1, device_id=giver(j), device_id_type=MESH)
     for other in (right, left, partner, across, mirror):
         pl.semaphore_signal(barrier, inc=1, device_id=other, device_id_type=MESH)
+    loads[1].wait()
     for j in range(QL):
-        chi_own[j] = bubble_ref[:, j]
-    vertex_copy.wait()
+        chi_own[j] = bubble[:, j]
+    loads[0].wait()
     for j in range(QL):
-        low[j] = vertex[:, j].astype(BF16)
+        low[j] = out_ref[:, j].astype(BF16)
     pl.semaphore_wait(barrier, 13)
 
     def rows_of(piece):
@@ -121,6 +129,8 @@
         copy1(s).start()
     for s in range(4):
         chi_copy(s, y).start()
+    for i in range(2, 6):
+        loads[i].start()
 
     for s in range(4):
         piece = piece_at(s, 0)
@@ -129,11 +139,14 @@
         pass_on(piece, send2.at[s, 1], left).start()
         pass_on(piece, send3.at[s, 0], partner).start()
 
+    loads[2].wait()
+    loads[3].wait()
+
     def select_rows(i, carry):
         at = pl.multiple_of(i * ROWS, ROWS)
         source = lax.broadcasted_iota(I32, (ROWS, K), 0) + at
         for c in range(2):
-            selector[c, pl.ds(at, ROWS), :] = one_hot(source == col_ref[c:c + 1, :])
+            selector[c, pl.ds(at, ROWS), :] = one_hot(source == cols_from[c:c + 1, :])
         return carry
 
     lax.fori_loop(0, K // ROWS, select_rows, 0)
@@ -144,7 +157,7 @@
     table_row = lax.broadcasted_iota(I32, (16, LANES), 0)
     table_lane = lax.broadcasted_iota(I32, (16, LANES), 1)
     for c in range(2):
-        table = row_ref[c]
+        table = rows_from[c]
         owner = table // (QL * K) * 32 + table % K // ROWS
         local = table // K % QL * ROWS + table % ROWS
         wanted = jnp.where(owner == me, local + 1, 0).astype(F32).astype(BF16)
@@ -315,8 +328,16 @@
     for h in range(2):
         for p in range(2):
             for q in range(QL):
-                home_ref[p, q, :, h * HALF:(h + 1) * HALF] = home[h, q, p]
-
+                out_ref[p, q, :, h * HALF:(h + 1) * HALF] += home[h, q, p].astype(F32)
+
+    stores = [
+        pltpu.make_async_copy(source, target, store.at[i])
+        for i, (source, target) in enumerate(((out_ref, to_ref), (out_a_ref, to_a_ref), (out_b_ref, to_b_ref)))
+    ]
+    stores[0].start()
+
+    loads[4].wait()
+    loads[5].wait()
     for h in range(2):
         others(h).wait_recv()
         own_copy(h).wait()
@@ -328,7 +349,7 @@
         lax.fori_loop(0, DEVS, unpack, 0, unroll=8)
         for b in range(4 * BLOCKS):
             lined_up[:, b * LANES:(b + 1) * LANES] = stage[pl.ds(b, DEVS, stride=TILE), :].astype(BF16)
-        for c, to_ref in enumerate((to_a_ref, to_b_ref)):
+        for c, sum_ref in enumerate((out_a_ref, out_b_ref)):
             for p in range(2):
                 rows = lined_up[:, (c * 2 + p) * HALF:(c * 2 + p + 1) * HALF]
                 placed[p * MINE:(p + 1) * MINE, :] = lax.dot_general(
@@ -339,28 +360,32 @@
                 moved = jnp.dot(
                     placed[...], selector[c, h * HALF:(h + 1) * HALF, cols], preferred_element_type=F32
                 )
-                moved = moved.reshape(2, QL, ROWS, NB)
-                if h == 0:
-                    to_ref[:, :, :, cols] = moved.astype(BF16)
-                else:
-                    to_ref[:, :, :, cols] = (to_ref[:, :, :, cols].astype(F32) + moved).astype(BF16)
-
+                sum_ref[:, :, :, cols] += moved.reshape(2, QL, ROWS, NB)
+            if h == 1:
+                stores[1 + c].start()
+
+    for copy in stores:
+        copy.wait()
     for h in range(2):
         others(h).wait_send()
         for s in range(4):
             home_copy(h, s).wait_send()
 
 
-def run_ladder(vertex, bubble, row_maps, col_maps):
-    vmem = pl.BlockSpec(memory_space=pltpu.VMEM)
-    out = jax.ShapeDtypeStruct((2, QL, ROWS, K), BF16)
+def run_ladder(vertex, cross_a, cross_b, bubble, row_maps, col_maps):
+    out = jax.ShapeDtypeStruct(vertex.shape, F32)
     return pl.pallas_call(
         ladder_kernel,
         out_shape=(out, out, out),
-        in_specs=[pl.BlockSpec(memory_space=pl.ANY), vmem, vmem, vmem],
-        out_specs=(vmem, vmem, vmem),
+        in_specs=[pl.BlockSpec(memory_space=pltpu.HBM)] * 6,
+        out_specs=(pl.BlockSpec(memory_space=pltpu.HBM),) * 3,
         scratch_shapes=[
             pltpu.VMEM((2, QL, ROWS, K), F32),
+            pltpu.VMEM((2, QL, ROWS, K), F32),
+            pltpu.VMEM((2, QL, ROWS, K), F32),
+            pltpu.VMEM((2, QL, K), F32),
+            pltpu.VMEM((2, 4 * QL, K), I32),
+            pltpu.VMEM((2, K), I32),
             pltpu.VMEM((QL, 2, ROWS, K), BF16),
             pltpu.VMEM((2, K, K), BF16),
             pltpu.VMEM((2, MINE, K), BF16),
@@ -378,7 +403,8 @@
             pltpu.VMEM((2, DEVS, TILE, LANES), BF16),
             pltpu.VMEM((DEVS, 4 * HALF), BF16),
             pltpu.VMEM((2 * MINE, HALF), BF16),
-            pltpu.SemaphoreType.DMA,
+            pltpu.SemaphoreType.DMA((6,)),
+            pltpu.SemaphoreType.DMA((3,)),
             pltpu.SemaphoreType.DMA((4,)),
             pltpu.SemaphoreType.DMA((4,)),
             pltpu.SemaphoreType.DMA((4,)),
@@ -394,18 +420,45 @@
             pltpu.SemaphoreType.REGULAR,
         ],
         compiler_params=pltpu.CompilerParams(
-            collective_id=0, has_side_effects=True, vmem_limit_bytes=28 * 2**20
+            collective_id=0, has_side_effects=True, vmem_limit_bytes=60 * 2**20
         ),
-    )(vertex, bubble, row_maps, col_maps)
-
-
-def per_device(vertex_ladder, vertex_cross_a, vertex_cross_b, bubble, row_maps, col_maps):
-    home, to_a, to_b = run_ladder(vertex_ladder, bubble, row_maps, col_maps)
-    return (
-        vertex_ladder + home.astype(F32),
-        vertex_cross_a + to_a.astype(F32),
-        vertex_cross_b + to_b.astype(F32),
-    )
+    )(vertex, cross_a, cross_b, bubble, row_maps, col_maps)
+
+
+def hand_over_kernel(*refs):
+    held, came, done = refs[6:]
+    blocks = [(i, p, q) for i in range(3) for p in range(2) for q in range(0, QL, 2)]
+
+    def bring(i, p, q):
+        return pltpu.make_async_copy(refs[i].at[p, q:q + 2], held.at[i, p, q:q + 2], came.at[i, p, q])
+
+    def write(i, p, q):
+        return pltpu.make_async_copy(held.at[i, p, q:q + 2], refs[3 + i].at[p, q:q + 2], done.at[i, p, q])
+
+    for block in blocks:
+        bring(*block).start()
+    for block in blocks:
+        bring(*block).wait()
+        write(*block).start()
+    for block in blocks:
+        write(*block).wait()
+
+
+def per_device(*args):
+    results = run_ladder(*args)
+    shape = jax.ShapeDtypeStruct(args[0].shape, F32)
+    return tuple(pl.pallas_call(
+        hand_over_kernel,
+        out_shape=(shape,) * 3,
+        in_specs=[pl.BlockSpec(memory_space=pltpu.HBM)] * 3,
+        out_specs=(pl.BlockSpec(memory_space=pltpu.HBM),) * 3,
+        scratch_shapes=[
+            pltpu.VMEM((3, 2, QL, ROWS, K), F32),
+            pltpu.SemaphoreType.DMA((3, 2, QL)),
+            pltpu.SemaphoreType.DMA((3, 2, QL)),
+        ],
+        compiler_params=pltpu.CompilerParams(vmem_limit_bytes=60 * 2**20),
+    )(*results))
 
 
 def solution(mesh):

time: 71.6 us -> 67.9 us (0.948)
  Pallas kernels: 63 us -> 67.1 us
  other arithmetic: 4.09 us -> 0 us
  local copies, waits for them, and re-layouts: 3.58 us -> 0 us
    add x2 -> x0, other arithmetic: 4.09 us -> none  [the longest x1 2.93 us: per_device(): vertex_cross_b + to_b.astype(F32)]
    unnamed x10 -> x0, local copies, waits for them, and re-layouts: 3.58 us -> none
    pallas_call x0 -> x1, Pallas kernels: none -> 3.03 us  [per_device(): pl.pallas_call(hand_over_kernel, out_shape=(shape,) * 3, in_specs=[pl.Blo...]
    pallas_call x1, Pallas kernels: 63 us -> 64.1 us  [run_ladder(): pl.pallas_call(ladder_kernel, out_shape=(out, out, out), in_specs=[pl.Blo...]
where the time goes in v5:
time: 67.9 us; the launch traced here: 67.8 us
  Pallas kernels  67.1 us (99%)
    pallas_call x1, Pallas kernels, run_ladder(): pl.pallas_call(ladder_kernel, out_shape=(out, out, out), in_specs=[pl.Blo...  64.1 us
    pallas_call x1, Pallas kernels, per_device(): pl.pallas_call(hand_over_kernel, out_shape=(shape,) * 3, in_specs=[pl.Blo...  3.03 us

profile of v5, /device:TPU:1, one launch (start us, length us, event | category | flops | bytes accessed | tf_op | source)
XLA Modules:
  0.0 67.8 jit_solution(7601628372649618148)
XLA Ops:
  0.6 64.1 %shard_map.85 = (f32[2,4,32,1024]{3,2,1,0:T(8,128)}, f32[2,4,32,1024]{3,2,1,0:T(8,128)}, f32[2,4,32,1024]{3,2,1,0:T(8,128)}) custom-call(f32[2,4,32,1024]{3,2,1,0:T(8,128)} %vertex_ref.1, f32[2,4,32,1024]{3,2,1,0:T(8,128)} %a_ref.1, f32[2,4,32,1024]{3,2,1,0:T(8,128)} %b_ref.1, f32[2,4,1024]{2,1,0:T(4,128)} %bubble_ref.1, s32[2,16,1024]{2,1,0:T(8,128)} %row_ref.1, ...), custom_call_target="tpu_custom_call" | custom-call | tf_op jit(solution)/shard_map/pallas_call | solution.py:377
  64.8 3.0 %shard_map.86 = (f32[2,4,32,1024]{3,2,1,0:T(8,128)}, f32[2,4,32,1024]{3,2,1,0:T(8,128)}, f32[2,4,32,1024]{3,2,1,0:T(8,128)}) custom-call(f32[2,4,32,1024]{3,2,1,0:T(8,128)} %get-tuple-element.6.refs_0_, f32[2,4,32,1024]{3,2,1,0:T(8,128)} %get-tuple-element.7.refs_1_, f32[2,4,32,1024]{3,2,1,0:T(8,128)} %get-tuple-element.8.refs_2_), custom_call_target="tpu_custom_call" | custom-call | tf_op jit(solution)/shard_map/pallas_call | solution.py:450

commit v6 on v5

--- a/solution.py
+++ b/solution.py
@@ -78,13 +78,13 @@
     def rows_of(piece):
         return pl.ds(pl.multiple_of(piece * ROWS, ROWS), ROWS)
 
-    def copy1(s):
+    def copy1(s, plane):
         j = (y + s) % 4
         return pltpu.make_async_remote_copy(
-            src_ref=low.at[j],
-            dst_ref=whole.at[:, rows_of(ka), :],
-            send_sem=send1.at[s],
-            recv_sem=recv.at[ka],
+            src_ref=low.at[j, plane],
+            dst_ref=whole.at[plane, rows_of(ka), :],
+            send_sem=send1.at[s, plane],
+            recv_sem=recv.at[plane, ka],
             device_id=taker(j),
             device_id_type=MESH,
         )
@@ -100,24 +100,13 @@
             device_id_type=MESH,
         )
 
-    def pass_on(piece, sem, target):
-        block = whole.at[:, rows_of(piece), :]
+    def pass_plane(piece, plane, sem, target):
+        block = whole.at[plane, rows_of(piece), :]
         return pltpu.make_async_remote_copy(
             src_ref=block,
             dst_ref=block,
             send_sem=sem,
-            recv_sem=recv.at[piece],
-            device_id=target,
-            device_id_type=MESH,
-        )
-
-    def pass_plane(piece, plane, sem, target):
-        block = whole.at[plane, rows_of(piece), :]
-        return pltpu.make_async_remote_copy(
-            src_ref=block,
-            dst_ref=block,
-            send_sem=sem,
-            recv_sem=recv.at[piece],
+            recv_sem=recv.at[plane, piece],
             device_id=target,
             device_id_type=MESH,
         )
@@ -126,19 +115,35 @@
         return (1 - core) * 16 + (y + 4 - s) % 4 * 4 + (x + shift) % 4
 
     for s in range(4):
-        copy1(s).start()
+        for plane in range(2):
+            copy1(s, plane).start()
     for s in range(4):
         chi_copy(s, y).start()
     for i in range(2, 6):
         loads[i].start()
 
-    for s in range(4):
+    def own_in(s):
         piece = piece_at(s, 0)
-        pass_on(piece, send2.at[s, 0], right).wait_recv()
-        pass_on(piece, send2.at[s, 0], right).start()
-        pass_on(piece, send2.at[s, 1], left).start()
-        pass_on(piece, send3.at[s, 0], partner).start()
-
+        for plane in range(2):
+            pass_plane(piece, plane, send2.at[s, plane], right).wait_recv()
+            pass_plane(piece, plane, send2.at[s, plane], right).start()
+            pass_plane(piece, plane, send2.at[s, 2 + plane], left).start()
+            pass_plane(piece, plane, send3.at[s, plane], partner).start()
+
+    def from_sides(s):
+        for plane in range(2):
+            for side, target in ((3, right), (1, left)):
+                piece = piece_at(s, side)
+                slot = 2 + side - 1 + plane
+                pass_plane(piece, plane, send3.at[s, slot], partner).wait_recv()
+                if (plane == 0) == (side == 3):
+                    pass_plane(piece, plane, send2.at[s, 4 + plane], target).start()
+                pass_plane(piece, plane, send3.at[s, slot], partner).start()
+
+    own_in(0)
+    own_in(1)
+    own_in(2)
+    own_in(3)
     loads[2].wait()
     loads[3].wait()
 
@@ -172,15 +177,10 @@
         device = lax.broadcasted_iota(I32, (DEVS, MINE), 0).astype(F32)
         place_order[c] = one_hot(device == owner)
 
-    for s in range(4):
-        piece = piece_at(s, 3)
-        pass_on(piece, send3.at[s, 1], partner).wait_recv()
-        pass_plane(piece, 0, send2.at[s, 2], right).start()
-        pass_on(piece, send3.at[s, 1], partner).start()
-        piece = piece_at(s, 1)
-        pass_on(piece, send3.at[s, 2], partner).wait_recv()
-        pass_plane(piece, 1, send2.at[s, 3], left).start()
-        pass_on(piece, send3.at[s, 2], partner).start()
+    from_sides(0)
+    from_sides(1)
+    from_sides(2)
+    from_sides(3)
 
     for s in range(4):
         chi_copy(s, s).wait_recv()
@@ -198,11 +198,13 @@
         left_even[MINE + at:MINE + at + ROWS, :] = im
 
     for s in range(4):
-        piece = piece_at(s, 2)
-        pass_on(piece, send3.at[s, 3], partner).wait_recv()
-        pass_on(piece, send3.at[s, 3], partner).start()
+        for plane in range(2):
+            piece = piece_at(s, 2)
+            pass_plane(piece, plane, send3.at[s, 6 + plane], partner).wait_recv()
+            pass_plane(piece, plane, send3.at[s, 6 + plane], partner).start()
     for i in range(16):
-        pass_on(core * 16 + i, send3.at[0, 0], partner).wait_recv()
+        for plane in range(2):
+            pass_plane(core * 16 + i, plane, send3.at[0, 0], partner).wait_recv()
     pl.semaphore_signal(known_half, inc=1, device_id=across, device_id_type=MESH)
 
     def product(left_op, n):
@@ -266,14 +268,13 @@
                 home_copy(h, s).start()
 
     for s in range(4):
-        copy1(s).wait_send()
         chi_copy(s, s).wait_send()
-        for t in range(2):
-            pass_on(piece_at(s, 0), send2.at[s, t], right).wait_send()
-        for t in range(2, 4):
+        for plane in range(2):
+            copy1(s, plane).wait_send()
+        for t in range(6):
             pass_plane(piece_at(s, 0), 0, send2.at[s, t], right).wait_send()
-        for t in range(4):
-            pass_on(piece_at(s, 0), send3.at[s, t], partner).wait_send()
+        for t in range(8):
+            pass_plane(piece_at(s, 0), 0, send3.at[s, t], partner).wait_send()
 
     def row_copy(h, target):
         return pltpu.make_async_remote_copy(
@@ -405,12 +406,12 @@
             pltpu.VMEM((2 * MINE, HALF), BF16),
             pltpu.SemaphoreType.DMA((6,)),
             pltpu.SemaphoreType.DMA((3,)),
+            pltpu.SemaphoreType.DMA((4, 2)),
             pltpu.SemaphoreType.DMA((4,)),
             pltpu.SemaphoreType.DMA((4,)),
-            pltpu.SemaphoreType.DMA((4,)),
-            pltpu.SemaphoreType.DMA((32,)),
-            pltpu.SemaphoreType.DMA((4, 4)),
-            pltpu.SemaphoreType.DMA((4, 4)),
+            pltpu.SemaphoreType.DMA((2, 32)),
+            pltpu.SemaphoreType.DMA((4, 6)),
+            pltpu.SemaphoreType.DMA((4, 8)),
             pltpu.SemaphoreType.DMA((2, 4)),
             pltpu.SemaphoreType.DMA((2, 4)),
             pltpu.SemaphoreType.DMA((2,)),

time: 67.9 us -> 67.4 us (level)
  no operation moved by 1% of the time
where the time goes in v6:
time: 67.4 us; the launch traced here: 67.2 us
  Pallas kernels  66.6 us (99%)
    pallas_call x1, Pallas kernels, run_ladder(): pl.pallas_call(ladder_kernel, out_shape=(out, out, out), in_specs=[pl.Blo...  63.5 us
    pallas_call x1, Pallas kernels, per_device(): pl.pallas_call(hand_over_kernel, out_shape=(shape,) * 3, in_specs=[pl.Blo...  3.03 us

profile of v6, /device:TPU:1, one launch (start us, length us, event | category | flops | bytes accessed | tf_op | source)
XLA Modules:
  0.0 67.2 jit_solution(8387556188065971350)
XLA Ops:
  0.6 63.5 %shard_map.85 = (f32[2,4,32,1024]{3,2,1,0:T(8,128)}, f32[2,4,32,1024]{3,2,1,0:T(8,128)}, f32[2,4,32,1024]{3,2,1,0:T(8,128)}) custom-call(f32[2,4,32,1024]{3,2,1,0:T(8,128)} %vertex_ref.1, f32[2,4,32,1024]{3,2,1,0:T(8,128)} %a_ref.1, f32[2,4,32,1024]{3,2,1,0:T(8,128)} %b_ref.1, f32[2,4,1024]{2,1,0:T(4,128)} %bubble_ref.1, s32[2,16,1024]{2,1,0:T(8,128)} %row_ref.1, ...), custom_call_target="tpu_custom_call" | custom-call | tf_op jit(solution)/shard_map/pallas_call | solution.py:378
  64.2 3.0 %shard_map.86 = (f32[2,4,32,1024]{3,2,1,0:T(8,128)}, f32[2,4,32,1024]{3,2,1,0:T(8,128)}, f32[2,4,32,1024]{3,2,1,0:T(8,128)}) custom-call(f32[2,4,32,1024]{3,2,1,0:T(8,128)} %get-tuple-element.6.refs_0_, f32[2,4,32,1024]{3,2,1,0:T(8,128)} %get-tuple-element.7.refs_1_, f32[2,4,32,1024]{3,2,1,0:T(8,128)} %get-tuple-element.8.refs_2_), custom_call_target="tpu_custom_call" | custom-call | tf_op jit(solution)/shard_map/pallas_call | solution.py:451

commit v7 on v6

--- a/solution.py
+++ b/solution.py
@@ -28,10 +28,10 @@
 
 
 def ladder_kernel(
-    vertex_ref, a_ref, b_ref, bubble_ref, row_ref, col_ref, to_ref, to_a_ref, to_b_ref,
-    out_ref, out_a_ref, out_b_ref, bubble, rows_from, cols_from, low, whole, base, left_even, left_odd, outgoing, home, chi_own, chi, selector, send_order, place_order,
+    vertex_ref, low, a_ref, b_ref, bubble, rows_from, cols_from, out_ref, out_a_ref, out_b_ref,
+    whole, base, left_even, left_odd, outgoing, home, chi_own, chi, selector, send_order, place_order,
     stage, packed, arrived, lined_up, placed,
-    load, store, send1, send_chi, recv_chi, recv, send2, send3, send_home, recv_home,
+    load, send1, send_chi, recv_chi, recv, send2, send3, send_home, recv_home,
     send_row, recv_row, own_row, known_half, known_all,
 ):
     pb, ka = lax.axis_index("pb"), lax.axis_index("ka")
@@ -54,25 +54,16 @@
 
     loads = [
         pltpu.make_async_copy(source, target, load.at[i])
-        for i, (source, target) in enumerate((
-            (vertex_ref, out_ref), (bubble_ref, bubble), (row_ref, rows_from), (col_ref, cols_from),
-            (a_ref, out_a_ref), (b_ref, out_b_ref),
-        ))
+        for i, (source, target) in enumerate(((vertex_ref, out_ref), (a_ref, out_a_ref), (b_ref, out_b_ref)))
     ]
-    loads[0].start()
-    loads[1].start()
     barrier = pltpu.get_barrier_semaphore()
     for j in range(4):
         pl.semaphore_signal(barrier, inc=1, device_id=taker(j), device_id_type=MESH)
         pl.semaphore_signal(barrier, inc=1, device_id=giver(j), device_id_type=MESH)
     for other in (right, left, partner, across, mirror):
         pl.semaphore_signal(barrier, inc=1, device_id=other, device_id_type=MESH)
-    loads[1].wait()
     for j in range(QL):
         chi_own[j] = bubble[:, j]
-    loads[0].wait()
-    for j in range(QL):
-        low[j] = out_ref[:, j].astype(BF16)
     pl.semaphore_wait(barrier, 13)
 
     def rows_of(piece):
@@ -81,7 +72,7 @@
     def copy1(s, plane):
         j = (y + s) % 4
         return pltpu.make_async_remote_copy(
-            src_ref=low.at[j, plane],
+            src_ref=low.at[plane, j],
             dst_ref=whole.at[plane, rows_of(ka), :],
             send_sem=send1.at[s, plane],
             recv_sem=recv.at[plane, ka],
@@ -119,8 +110,8 @@
             copy1(s, plane).start()
     for s in range(4):
         chi_copy(s, y).start()
-    for i in range(2, 6):
-        loads[i].start()
+    for copy in loads:
+        copy.start()
 
     def own_in(s):
         piece = piece_at(s, 0)
@@ -144,8 +135,6 @@
     own_in(1)
     own_in(2)
     own_in(3)
-    loads[2].wait()
-    loads[3].wait()
 
     def select_rows(i, carry):
         at = pl.multiple_of(i * ROWS, ROWS)
@@ -326,19 +315,13 @@
         lax.fori_loop(1, DEVS, send, 0)
         own_copy(h).start()
 
+    for copy in loads:
+        copy.wait()
     for h in range(2):
         for p in range(2):
             for q in range(QL):
                 out_ref[p, q, :, h * HALF:(h + 1) * HALF] += home[h, q, p].astype(F32)
 
-    stores = [
-        pltpu.make_async_copy(source, target, store.at[i])
-        for i, (source, target) in enumerate(((out_ref, to_ref), (out_a_ref, to_a_ref), (out_b_ref, to_b_ref)))
-    ]
-    stores[0].start()
-
-    loads[4].wait()
-    loads[5].wait()
     for h in range(2):
         others(h).wait_recv()
         own_copy(h).wait()
@@ -362,11 +345,7 @@
                     placed[...], selector[c, h * HALF:(h + 1) * HALF, cols], preferred_element_type=F32
                 )
                 sum_ref[:, :, :, cols] += moved.reshape(2, QL, ROWS, NB)
-            if h == 1:
-                stores[1 + c].start()
-
-    for copy in stores:
-        copy.wait()
+
     for h in range(2):
         others(h).wait_send()
         for s in range(4):
@@ -375,19 +354,13 @@
 
 def run_ladder(vertex, cross_a, cross_b, bubble, row_maps, col_maps):
     out = jax.ShapeDtypeStruct(vertex.shape, F32)
+    hbm, vmem = pl.BlockSpec(memory_space=pltpu.HBM), pl.BlockSpec(memory_space=pltpu.VMEM)
     return pl.pallas_call(
         ladder_kernel,
         out_shape=(out, out, out),
-        in_specs=[pl.BlockSpec(memory_space=pltpu.HBM)] * 6,
-        out_specs=(pl.BlockSpec(memory_space=pltpu.HBM),) * 3,
+        in_specs=[hbm, vmem, hbm, hbm, vmem, vmem, vmem],
+        out_specs=(vmem, vmem, vmem),
         scratch_shapes=[
-            pltpu.VMEM((2, QL, ROWS, K), F32),
-            pltpu.VMEM((2, QL, ROWS, K), F32),
-            pltpu.VMEM((2, QL, ROWS, K), F32),
-            pltpu.VMEM((2, QL, K), F32),
-            pltpu.VMEM((2, 4 * QL, K), I32),
-            pltpu.VMEM((2, K), I32),
-            pltpu.VMEM((QL, 2, ROWS, K), BF16),
             pltpu.VMEM((2, K, K), BF16),
             pltpu.VMEM((2, MINE, K), BF16),
             pltpu.VMEM((2 * MINE, K), BF16),
@@ -404,7 +377,6 @@
             pltpu.VMEM((2, DEVS, TILE, LANES), BF16),
             pltpu.VMEM((DEVS, 4 * HALF), BF16),
             pltpu.VMEM((2 * MINE, HALF), BF16),
-            pltpu.SemaphoreType.DMA((6,)),
             pltpu.SemaphoreType.DMA((3,)),
             pltpu.SemaphoreType.DMA((4, 2)),
             pltpu.SemaphoreType.DMA((4,)),
@@ -421,28 +393,21 @@
             pltpu.SemaphoreType.REGULAR,
         ],
         compiler_params=pltpu.CompilerParams(
-            collective_id=0, has_side_effects=True, vmem_limit_bytes=60 * 2**20
+            collective_id=0, has_side_effects=True, vmem_limit_bytes=50 * 2**20
         ),
-    )(vertex, cross_a, cross_b, bubble, row_maps, col_maps)
+    )(vertex, vertex.astype(BF16), cross_a, cross_b, bubble, row_maps, col_maps)
 
 
 def hand_over_kernel(*refs):
-    held, came, done = refs[6:]
-    blocks = [(i, p, q) for i in range(3) for p in range(2) for q in range(0, QL, 2)]
-
-    def bring(i, p, q):
-        return pltpu.make_async_copy(refs[i].at[p, q:q + 2], held.at[i, p, q:q + 2], came.at[i, p, q])
-
-    def write(i, p, q):
-        return pltpu.make_async_copy(held.at[i, p, q:q + 2], refs[3 + i].at[p, q:q + 2], done.at[i, p, q])
-
-    for block in blocks:
-        bring(*block).start()
-    for block in blocks:
-        bring(*block).wait()
-        write(*block).start()
-    for block in blocks:
-        write(*block).wait()
+    done = refs[-1]
+    copies = [
+        pltpu.make_async_copy(refs[i].at[p], refs[3 + i].at[p], done.at[i, p])
+        for i in range(3) for p in range(2)
+    ]
+    for copy in copies:
+        copy.start()
+    for copy in copies:
+        copy.wait()
 
 
 def per_device(*args):
@@ -451,14 +416,10 @@
     return tuple(pl.pallas_call(
         hand_over_kernel,
         out_shape=(shape,) * 3,
-        in_specs=[pl.BlockSpec(memory_space=pltpu.HBM)] * 3,
+        in_specs=[pl.BlockSpec(memory_space=pltpu.VMEM)] * 3,
         out_specs=(pl.BlockSpec(memory_space=pltpu.HBM),) * 3,
-        scratch_shapes=[
-            pltpu.VMEM((3, 2, QL, ROWS, K), F32),
-            pltpu.SemaphoreType.DMA((3, 2, QL)),
-            pltpu.SemaphoreType.DMA((3, 2, QL)),
-        ],
-        compiler_params=pltpu.CompilerParams(vmem_limit_bytes=60 * 2**20),
+        scratch_shapes=[pltpu.SemaphoreType.DMA((3, 2))],
+        compiler_params=pltpu.CompilerParams(vmem_limit_bytes=50 * 2**20),
     )(*results))
 
 

time: 67.4 us -> 66.4 us (0.985)
  Pallas kernels: 66.6 us -> 64.2 us
  other arithmetic: 0 us -> 1.33 us
    convert_element_type x0 -> x1, other arithmetic: none -> 1.33 us  [run_ladder(): vertex.astype(BF16)]
    pallas_call x1, Pallas kernels: 3.03 us -> 1.71 us  [per_device(): pl.pallas_call(hand_over_kernel, out_shape=(shape,) * 3, in_specs=[pl.Blo...]
    pallas_call x1, Pallas kernels: 63.5 us -> 62.5 us  [run_ladder(): pl.pallas_call(ladder_kernel, out_shape=(out, out, out), in_specs=[hbm, v...]
where the time goes in v7:
time: 66.4 us; the launch traced here: 66.2 us
  Pallas kernels  64.2 us (97%)
  other arithmetic  1.33 us (2%)
  between operations  0.69 us (1%)
    pallas_call x1, Pallas kernels, run_ladder(): pl.pallas_call(ladder_kernel, out_shape=(out, out, out), in_specs=[hbm, v...  62.5 us
    pallas_call x1, Pallas kernels, per_device(): pl.pallas_call(hand_over_kernel, out_shape=(shape,) * 3, in_specs=[pl.Blo...  1.71 us
    convert_element_type x1, other arithmetic, run_ladder(): vertex.astype(BF16)  1.33 us

profile of v7, /device:TPU:1, one launch (start us, length us, event | category | flops | bytes accessed | tf_op | source)
XLA Modules:
  0.0 66.2 jit_solution(11668125005594894219)
XLA Ops:
  0.6 0.0 copy-start.2
  0.6 0.0 copy-start
  0.7 0.0 copy-start.1
  0.7 1.3 %convert_element_type.3.low = bf16[2,4,32,1024]{3,2,1,0:T(8,128)(2,1)S(1)} convert(f32[2,4,32,1024]{3,2,1,0:T(8,128)} %vertex_ref.1) | non-fusion elementwise | flops 262144 | bytes 1572864 | tf_op jit(solution)/shard_map/convert_element_type | solution.py:398
  2.0 0.0 copy-done.2
  2.0 0.0 copy-done
  2.0 0.0 copy-done.1
  2.0 62.5 %shard_map.85 = (f32[2,4,32,1024]{3,2,1,0:T(8,128)S(1)}, f32[2,4,32,1024]{3,2,1,0:T(8,128)S(1)}, f32[2,4,32,1024]{3,2,1,0:T(8,128)S(1)}) custom-call(f32[2,4,32,1024]{3,2,1,0:T(8,128)} %vertex_ref.1, bf16[2,4,32,1024]{3,2,1,0:T(8,128)(2,1)S(1)} %convert_element_type.3.low, f32[2,4,32,1024]{3,2,1,0:T(8,128)} %a_ref.1, f32[2,4,32,1024]{3,2,1,0:T(8,128)} %b_ref.1, ...), custom_call_target="tpu_custom_call" | custom-call | tf_op jit(solution)/shard_map/pallas_call | solution.py:358
  64.5 1.7 %shard_map.86 = (f32[2,4,32,1024]{3,2,1,0:T(8,128)}, f32[2,4,32,1024]{3,2,1,0:T(8,128)}, f32[2,4,32,1024]{3,2,1,0:T(8,128)}) custom-call(f32[2,4,32,1024]{3,2,1,0:T(8,128)S(1)} %get-tuple-element.6.refs_0_, f32[2,4,32,1024]{3,2,1,0:T(8,128)S(1)} %get-tuple-element.7.refs_1_, f32[2,4,32,1024]{3,2,1,0:T(8,128)S(1)} %get-tuple-element.8.refs_2_), custom_call_target="tpu_custom_call" | custom-call | tf_op jit(solution)/shard_map/pallas_call | solution.py:416
Async XLA Ops:
  0.6 1.4 %copy-start.2 = (s32[2,1024]{1,0:T(2,128)S(1)}, s32[2,1024]{1,0:T(2,128)}, u32[]{:S(2)}) copy-start(s32[2,1024]{1,0:T(2,128)} %cols_from.1) | copy-start | bytes 24580
  0.6 1.4 %copy-start = (s32[2,16,1024]{2,1,0:T(8,128)S(1)}, s32[2,16,1024]{2,1,0:T(8,128)}, u32[]{:S(2)}) copy-start(s32[2,16,1024]{2,1,0:T(8,128)} %rows_from.1) | copy-start | bytes 393220
  0.7 1.4 %copy-start.1 = (f32[2,4,1024]{2,1,0:T(4,128)S(1)}, f32[2,4,1024]{2,1,0:T(4,128)}, u32[]{:S(2)}) copy-start(f32[2,4,1024]{2,1,0:T(4,128)} %bubble.1) | copy-start | bytes 98308

commit v8 on v7

--- a/solution.py
+++ b/solution.py
@@ -130,11 +130,6 @@
                 if (plane == 0) == (side == 3):
                     pass_plane(piece, plane, send2.at[s, 4 + plane], target).start()
                 pass_plane(piece, plane, send3.at[s, slot], partner).start()
-
-    own_in(0)
-    own_in(1)
-    own_in(2)
-    own_in(3)
 
     def select_rows(i, carry):
         at = pl.multiple_of(i * ROWS, ROWS)
@@ -166,6 +161,11 @@
         device = lax.broadcasted_iota(I32, (DEVS, MINE), 0).astype(F32)
         place_order[c] = one_hot(device == owner)
 
+    own_in(0)
+    own_in(1)
+    own_in(2)
+    own_in(3)
+
     from_sides(0)
     from_sides(1)
     from_sides(2)
@@ -302,17 +302,17 @@
                         c * DEVS:(c + 1) * DEVS, b * LANES:(b + 1) * LANES
                     ]
 
-        def pack(t, carry):
+        def pack(t):
             packed[h, t] = stage[pl.ds(pl.multiple_of(t * TILE, TILE), TILE), :].astype(BF16)
+
+        def send(i, carry):
+            target = (me + i) % DEVS
+            pack(target)
+            row_copy(h, target).start()
             return carry
 
-        lax.fori_loop(0, DEVS, pack, 0, unroll=8)
-
-        def send(i, carry):
-            row_copy(h, (me + i) % DEVS).start()
-            return carry
-
         lax.fori_loop(1, DEVS, send, 0)
+        pack(me)
         own_copy(h).start()
 
     for copy in loads:

time: 66.4 us -> 66.3 us (level)
  no operation moved by 1% of the time
where the time goes in v8:
time: 66.3 us; the launch traced here: 66.1 us
  Pallas kernels  64.1 us (97%)
  other arithmetic  1.33 us (2%)
  between operations  0.69 us (1%)
    pallas_call x1, Pallas kernels, run_ladder(): pl.pallas_call(ladder_kernel, out_shape=(out, out, out), in_specs=[hbm, v...  62.4 us
    pallas_call x1, Pallas kernels, per_device(): pl.pallas_call(hand_over_kernel, out_shape=(shape,) * 3, in_specs=[pl.Blo...  1.71 us
    convert_element_type x1, other arithmetic, run_ladder(): vertex.astype(BF16)  1.33 us

profile of v8, /device:TPU:1, one launch (start us, length us, event | category | flops | bytes accessed | tf_op | source)
XLA Modules:
  0.0 66.1 jit_solution(16154739244096749126)
XLA Ops:
  0.6 0.0 copy-start.2
  0.6 0.0 copy-start
  0.7 0.0 copy-start.1
  0.7 1.3 %convert_element_type.3.low = bf16[2,4,32,1024]{3,2,1,0:T(8,128)(2,1)S(1)} convert(f32[2,4,32,1024]{3,2,1,0:T(8,128)} %vertex_ref.1) | non-fusion elementwise | flops 262144 | bytes 1572864 | tf_op jit(solution)/shard_map/convert_element_type | solution.py:398
  2.0 0.0 copy-done.2
  2.0 0.0 copy-done
  2.0 0.0 copy-done.1
  2.0 62.4 %shard_map.85 = (f32[2,4,32,1024]{3,2,1,0:T(8,128)S(1)}, f32[2,4,32,1024]{3,2,1,0:T(8,128)S(1)}, f32[2,4,32,1024]{3,2,1,0:T(8,128)S(1)}) custom-call(f32[2,4,32,1024]{3,2,1,0:T(8,128)} %vertex_ref.1, bf16[2,4,32,1024]{3,2,1,0:T(8,128)(2,1)S(1)} %convert_element_type.3.low, f32[2,4,32,1024]{3,2,1,0:T(8,128)} %a_ref.1, f32[2,4,32,1024]{3,2,1,0:T(8,128)} %b_ref.1, ...), custom_call_target="tpu_custom_call" | custom-call | tf_op jit(solution)/shard_map/pallas_call | solution.py:358
  64.4 1.7 %shard_map.86 = (f32[2,4,32,1024]{3,2,1,0:T(8,128)}, f32[2,4,32,1024]{3,2,1,0:T(8,128)}, f32[2,4,32,1024]{3,2,1,0:T(8,128)}) custom-call(f32[2,4,32,1024]{3,2,1,0:T(8,128)S(1)} %get-tuple-element.6.refs_0_, f32[2,4,32,1024]{3,2,1,0:T(8,128)S(1)} %get-tuple-element.7.refs_1_, f32[2,4,32,1024]{3,2,1,0:T(8,128)S(1)} %get-tuple-element.8.refs_2_), custom_call_target="tpu_custom_call" | custom-call | tf_op jit(solution)/shard_map/pallas_call | solution.py:416
Async XLA Ops:
  0.6 1.4 %copy-start.2 = (s32[2,1024]{1,0:T(2,128)S(1)}, s32[2,1024]{1,0:T(2,128)}, u32[]{:S(2)}) copy-start(s32[2,1024]{1,0:T(2,128)} %cols_from.1) | copy-start | bytes 24580
  0.6 1.4 %copy-start = (s32[2,16,1024]{2,1,0:T(8,128)S(1)}, s32[2,16,1024]{2,1,0:T(8,128)}, u32[]{:S(2)}) copy-start(s32[2,16,1024]{2,1,0:T(8,128)} %rows_from.1) | copy-start | bytes 393220
  0.7 1.4 %copy-start.1 = (f32[2,4,1024]{2,1,0:T(4,128)S(1)}, f32[2,4,1024]{2,1,0:T(4,128)}, u32[]{:S(2)}) copy-start(f32[2,4,1024]{2,1,0:T(4,128)} %bubble.1) | copy-start | bytes 98308

commit v9 on v8

--- a/solution.py
+++ b/solution.py
@@ -110,8 +110,6 @@
             copy1(s, plane).start()
     for s in range(4):
         chi_copy(s, y).start()
-    for copy in loads:
-        copy.start()
 
     def own_in(s):
         piece = piece_at(s, 0)
@@ -165,6 +163,8 @@
     own_in(1)
     own_in(2)
     own_in(3)
+    for copy in loads:
+        copy.start()
 
     from_sides(0)
     from_sides(1)

time: 66.3 us -> 66.3 us (level)
  no operation moved by 1% of the time
where the time goes in v9:
time: 66.3 us; the launch traced here: 66.1 us
  Pallas kernels  64.1 us (97%)
  other arithmetic  1.33 us (2%)
  between operations  0.69 us (1%)
    pallas_call x1, Pallas kernels, run_ladder(): pl.pallas_call(ladder_kernel, out_shape=(out, out, out), in_specs=[hbm, v...  62.4 us
    pallas_call x1, Pallas kernels, per_device(): pl.pallas_call(hand_over_kernel, out_shape=(shape,) * 3, in_specs=[pl.Blo...  1.71 us
    convert_element_type x1, other arithmetic, run_ladder(): vertex.astype(BF16)  1.33 us

profile of v9, /device:TPU:1, one launch (start us, length us, event | category | flops | bytes accessed | tf_op | source)
XLA Modules:
  0.0 66.1 jit_solution(7460387987596548847)
XLA Ops:
  0.6 0.0 copy-start.2
  0.6 0.0 copy-start
  0.7 0.0 copy-start.1
  0.7 1.3 %convert_element_type.3.low = bf16[2,4,32,1024]{3,2,1,0:T(8,128)(2,1)S(1)} convert(f32[2,4,32,1024]{3,2,1,0:T(8,128)} %vertex_ref.1) | non-fusion elementwise | flops 262144 | bytes 1572864 | tf_op jit(solution)/shard_map/convert_element_type | solution.py:398
  2.0 0.0 copy-done.2
  2.0 0.0 copy-done
  2.0 0.0 copy-done.1
  2.0 62.4 %shard_map.85 = (f32[2,4,32,1024]{3,2,1,0:T(8,128)S(1)}, f32[2,4,32,1024]{3,2,1,0:T(8,128)S(1)}, f32[2,4,32,1024]{3,2,1,0:T(8,128)S(1)}) custom-call(f32[2,4,32,1024]{3,2,1,0:T(8,128)} %vertex_ref.1, bf16[2,4,32,1024]{3,2,1,0:T(8,128)(2,1)S(1)} %convert_element_type.3.low, f32[2,4,32,1024]{3,2,1,0:T(8,128)} %a_ref.1, f32[2,4,32,1024]{3,2,1,0:T(8,128)} %b_ref.1, ...), custom_call_target="tpu_custom_call" | custom-call | tf_op jit(solution)/shard_map/pallas_call | solution.py:358
  64.4 1.7 %shard_map.86 = (f32[2,4,32,1024]{3,2,1,0:T(8,128)}, f32[2,4,32,1024]{3,2,1,0:T(8,128)}, f32[2,4,32,1024]{3,2,1,0:T(8,128)}) custom-call(f32[2,4,32,1024]{3,2,1,0:T(8,128)S(1)} %get-tuple-element.6.refs_0_, f32[2,4,32,1024]{3,2,1,0:T(8,128)S(1)} %get-tuple-element.7.refs_1_, f32[2,4,32,1024]{3,2,1,0:T(8,128)S(1)} %get-tuple-element.8.refs_2_), custom_call_target="tpu_custom_call" | custom-call | tf_op jit(solution)/shard_map/pallas_call | solution.py:416
Async XLA Ops:
  0.6 1.4 %copy-start.2 = (s32[2,1024]{1,0:T(2,128)S(1)}, s32[2,1024]{1,0:T(2,128)}, u32[]{:S(2)}) copy-start(s32[2,1024]{1,0:T(2,128)} %cols_from.1) | copy-start | bytes 24580
  0.6 1.4 %copy-start = (s32[2,16,1024]{2,1,0:T(8,128)S(1)}, s32[2,16,1024]{2,1,0:T(8,128)}, u32[]{:S(2)}) copy-start(s32[2,16,1024]{2,1,0:T(8,128)} %rows_from.1) | copy-start | bytes 393220
  0.7 1.4 %copy-start.1 = (f32[2,4,1024]{2,1,0:T(4,128)S(1)}, f32[2,4,1024]{2,1,0:T(4,128)}, u32[]{:S(2)}) copy-start(f32[2,4,1024]{2,1,0:T(4,128)} %bubble.1) | copy-start | bytes 98308
